TPU v7x, 256 devices: a whole 4x4x8 slice. The times are simulated.
256 devices in a mesh: tower: 16 (over z, x_hi), plate: 16 (over y, x_lo, core).
Axes of the slice: x: 4 (x_hi: 2, x_lo: 2; x = x_hi * 2 + x_lo), y: 4, z: 8, core: 2. Of those that a mesh axis runs over, the one named last changes fastest.
Arguments:
- features: bfloat16 [16, 4096, 128], P('tower', 'plate'), may hold values from -6 to 6
- adjoint: bfloat16 [16, 4096, 128], P('tower', 'plate'), may hold values from -6 to 6
- positions: bfloat16 [3, 16, 4096], P(None, 'tower', 'plate'), may hold values from 0 to 1
- w_rbf: bfloat16 [16, 128], replicated, may hold values from -1.5 to 1.5
- b_rbf: float32 [128], replicated, may hold values from -1 to 1
- w_filter: bfloat16 [128, 128], replicated, may hold values from -0.5 to 0.5
- b_filter: float32 [128], replicated, may hold values from -1 to 1
- atom_counts: int32 [16, 16], P('tower', 'plate'), may hold values from 128 to 256, as said below
- tile_counts: int32 [16, 16], P('tower', 'plate'), may hold values from 1 to 56, as said below
- tower_tiles: int32 [16, 16, 56], P('tower', 'plate'), may hold values from 0 to 23
- plate_tiles: int32 [16, 16, 56], P('tower', 'plate'), may hold values from 0 to 127
- image_shifts: int32 [16, 16, 56], P('tower', 'plate'), may hold values from 0 to 8
Outputs:
- grad_features: float32 [16, 4096, 128], P('tower', 'plate')
- grad_positions: float32 [3, 16, 4096], P(None, 'tower', 'plate')
- grad_w_rbf: float32 [16, 128], replicated
- grad_b_rbf: float32 [128], replicated
- grad_w_filter: float32 [128, 128], replicated
- grad_b_filter: float32 [128], replicated
Inputs may be any that keep to these rules, and one draw needn't show every extreme that they name: `atom_counts`: 256 in at least one brick. `tile_counts`: 56 in at least one brick; entries past the count are unused. `tower_tiles`: tiles below 8 lie in the brick below, the next 8 in the brick itself, the rest in the brick above. `plate_tiles`: tile v lies in brick v // 8 of the same plate. `image_shifts`: shift c moves the receiver by c // 3 - 1 along x and c % 3 - 1 along y.
All inputs are finite; a program needn't handle non-finite values.
Results may differ from a plain program's by a relative error of at most 0.005.
Values may be sent and summed in bfloat16 or wider, within the bound.
A program may use at most 64 MiB of HBM per device.

v0:
```python
import math

import jax
import jax.numpy as jnp
from jax import lax
from jax.sharding import PartitionSpec as P

TILE = 32


box_side = 1.0
brick_height = 1.0
cutoff_radius = 3.0
soften = 0.01
sharpness = 10.0
log_two = math.log(2.0)


def shifted(block, axis, distance):
    devices = range(lax.axis_size(axis))
    route = [((i - distance) % len(devices), i) for i in devices]
    return lax.ppermute(block, axis, route)


def shift_vector(shift_code, tower_tile, per_brick):
    step_z = tower_tile // per_brick - 1
    return jnp.stack(
        [
            (shift_code // 3 - 1).astype(jnp.float32) * box_side,
            (shift_code % 3 - 1).astype(jnp.float32) * box_side,
            step_z.astype(jnp.float32) * brick_height,
        ]
    )


def pair_tile(adj_rows, recv_pos, feat_rows, send_pos, shift_vec, w_rbf, b_rbf, w_filter, b_filter):
    size_recv = adj_rows.shape[0]
    size_send = feat_rows.shape[0]
    feat_width = adj_rows.shape[1]
    displace = recv_pos[:, :, None] + shift_vec[:, None, None] - send_pos[:, None, :]
    distance = jnp.sqrt(jnp.sum(displace * displace, axis=0) + soften).reshape(-1)
    nbasis = w_rbf.shape[0]
    centres = jnp.arange(nbasis, dtype=jnp.float32) * (cutoff_radius / (nbasis - 1))
    offsets = distance[None, :] - centres[:, None]
    basis = jnp.exp(-sharpness * offsets * offsets)
    basis_b = basis.astype(jnp.bfloat16)
    preact = (
        lax.dot_general(
            basis_b, w_rbf, (((0,), (0,)), ((), ())), preferred_element_type=jnp.float32
        )
        + b_rbf
    )
    softed = (jax.nn.softplus(preact) - log_two).astype(jnp.bfloat16)
    filter_raw = jnp.dot(softed, w_filter, preferred_element_type=jnp.float32) + b_filter
    inside = distance < cutoff_radius
    phase_arg = math.pi / cutoff_radius * distance
    envelope = jnp.where(inside, 0.5 * (jnp.cos(phase_arg) + 1.0), 0.0)
    slope = jnp.where(inside, -0.5 * (math.pi / cutoff_radius) * jnp.sin(phase_arg), 0.0)
    adj_wide = adj_rows.astype(jnp.float32)
    feat_wide = feat_rows.astype(jnp.float32)
    filtered = (filter_raw * envelope[:, None]).reshape(size_recv, size_send, feat_width)
    grad_rows = jnp.einsum("if,ijf->jf", adj_wide, filtered)
    adjoint_pair = (adj_wide[:, None, :] * feat_wide[None, :, :]).reshape(
        size_recv * size_send, feat_width
    )
    d_raw = adjoint_pair * envelope[:, None]
    d_raw_b = d_raw.astype(jnp.bfloat16)
    grad_bf = jnp.sum(d_raw, axis=0)
    grad_wf = lax.dot_general(
        softed, d_raw_b, (((0,), (0,)), ((), ())), preferred_element_type=jnp.float32
    )
    d_soft = lax.dot_general(
        d_raw_b, w_filter, (((1,), (1,)), ((), ())), preferred_element_type=jnp.float32
    )
    d_pre = d_soft * jax.nn.sigmoid(preact)
    d_pre_b = d_pre.astype(jnp.bfloat16)
    grad_br = jnp.sum(d_pre, axis=0)
    grad_wr = lax.dot_general(
        basis_b, d_pre_b, (((1,), (0,)), ((), ())), preferred_element_type=jnp.float32
    )
    d_basis = lax.dot_general(
        w_rbf, d_pre_b, (((1,), (1,)), ((), ())), preferred_element_type=jnp.float32
    )
    d_dist = jnp.sum(d_basis * basis * (-2.0 * sharpness) * offsets, axis=0)
    d_dist = d_dist + jnp.sum(adjoint_pair * filter_raw, axis=1) * slope
    radial = (d_dist / distance).reshape(size_recv, size_send)
    pull = displace * radial[None]
    return (
        grad_rows,
        jnp.sum(pull, axis=2),
        -jnp.sum(pull, axis=1),
        (grad_wr, grad_br, grad_wf, grad_bf),
    )


def add_into(array, piece, starts):
    current = lax.dynamic_slice(array, starts, piece.shape)
    return lax.dynamic_update_slice(array, current + piece, starts)


def add_weights(left, right):
    return jax.tree.map(lambda first_term, second_term: first_term + second_term, left, right)


def local(
    features,
    adjoint,
    positions,
    w_rbf,
    b_rbf,
    w_filter,
    b_filter,
    atom_counts,
    tile_counts,
    tower_tiles,
    plate_tiles,
    image_shifts,
):
    brick_atoms = features.shape[1]
    feat_width = features.shape[2]
    tile_size = TILE
    per_brick = brick_atoms // tile_size
    plate_count = lax.axis_size("plate")
    zero_i = jnp.int32(0)
    live_mask = jnp.arange(brick_atoms, dtype=jnp.int32) < atom_counts[0, 0]
    zero_b = jnp.zeros((), jnp.bfloat16)
    own_feat = jnp.where(live_mask[:, None], features[0], zero_b)
    own_adj = jnp.where(live_mask[:, None], adjoint[0], zero_b)
    own_pos = positions[:, 0, :]
    from_below = shifted((own_adj, own_pos), "tower", 1)
    from_above = shifted((own_adj, own_pos), "tower", -1)
    tower_adj = jnp.concatenate([from_below[0], own_adj, from_above[0]], axis=0)
    tower_pos_b = jnp.concatenate([from_below[1], own_pos, from_above[1]], axis=1)
    tower_pos = tower_pos_b.astype(jnp.float32)
    weight_zero = (
        jnp.zeros(w_rbf.shape, jnp.float32),
        jnp.zeros(b_rbf.shape, jnp.float32),
        jnp.zeros(w_filter.shape, jnp.float32),
        jnp.zeros(b_filter.shape, jnp.float32),
    )
    plate_feat, plate_pos_b = (
        lax.all_gather(own_feat, "plate", axis=0, tiled=True),
        lax.all_gather(own_pos, "plate", axis=1, tiled=True),
    )
    plate_pos = plate_pos_b.astype(jnp.float32)

    def visit_listed(entry, totals):
        acc_dh, acc_gp, acc_tower, acc_weights = totals
        tower_tile = tower_tiles[0, 0, entry]
        plate_tile = plate_tiles[0, 0, entry]
        recv_start = tower_tile * tile_size
        send_start = plate_tile * tile_size
        adj_rows = lax.dynamic_slice_in_dim(tower_adj, recv_start, tile_size, 0)
        recv_pos = lax.dynamic_slice_in_dim(tower_pos, recv_start, tile_size, 1)
        feat_rows = lax.dynamic_slice_in_dim(plate_feat, send_start, tile_size, 0)
        send_pos = lax.dynamic_slice_in_dim(plate_pos, send_start, tile_size, 1)
        shift_vec = shift_vector(image_shifts[0, 0, entry], tower_tile, per_brick)
        grad_rows, grad_recv, grad_send, grad_weights = pair_tile(
            adj_rows, recv_pos, feat_rows, send_pos, shift_vec, w_rbf, b_rbf, w_filter, b_filter
        )
        brick_index = plate_tile // per_brick
        local_start = plate_tile % per_brick * tile_size
        acc_dh = add_into(acc_dh, grad_rows[None], (brick_index, local_start, zero_i))
        acc_gp = add_into(acc_gp, grad_send[None], (brick_index, zero_i, local_start))
        acc_tower = add_into(acc_tower, grad_recv, (zero_i, recv_start))
        return (acc_dh, acc_gp, acc_tower, add_weights(acc_weights, grad_weights))

    initial = (
        jnp.zeros((plate_count, brick_atoms, feat_width), jnp.float32),
        jnp.zeros((plate_count, 3, brick_atoms), jnp.float32),
        jnp.zeros((3, 3 * brick_atoms), jnp.float32),
        weight_zero,
    )
    acc_dh, acc_gp, tower_grad, acc_weights = lax.fori_loop(
        0, tile_counts[0, 0], visit_listed, initial
    )
    home_dh, home_gp = (
        lax.psum_scatter(acc_dh, "plate", scatter_dimension=0, tiled=True),
        lax.psum_scatter(acc_gp, "plate", scatter_dimension=0, tiled=True),
    )
    plate_dh = home_dh[0]
    plate_gp = home_gp[0]
    back_down = shifted(tower_grad[:, :brick_atoms], "tower", -1)
    back_up = shifted(tower_grad[:, 2 * brick_atoms :], "tower", 1)
    total_pos = plate_gp + tower_grad[:, brick_atoms : 2 * brick_atoms] + back_down + back_up
    tile_total = tile_counts[0, 0].astype(jnp.float32)
    summed = lax.psum(
        (acc_weights[0], acc_weights[1], acc_weights[2], acc_weights[3], tile_total),
        ("tower", "plate"),
    )
    scale = lax.rsqrt(summed[4] * (tile_size * tile_size))
    grad_features = jnp.where(live_mask[:, None], plate_dh, 0.0)[None]
    grad_positions = total_pos.reshape(3, 1, brick_atoms)
    return (
        grad_features,
        grad_positions,
        summed[0] * scale,
        summed[1] * scale,
        summed[2] * scale,
        summed[3] * scale,
    )


def solution(mesh):
    in_specs = (
        P("tower", "plate", None),
        P("tower", "plate", None),
        P(None, "tower", "plate"),
        P(),
        P(),
        P(),
        P(),
        P("tower", "plate"),
        P("tower", "plate"),
        P("tower", "plate", None),
        P("tower", "plate", None),
        P("tower", "plate", None),
    )
    out_specs = (P("tower", "plate", None), P(None, "tower", "plate"), P(), P(), P(), P())
    return jax.shard_map(local, mesh=mesh, in_specs=in_specs, out_specs=out_specs, check_vma=False)
```

profile of v0, /device:TPU:1, one launch (start us, length us, event | category | flops | bytes accessed | tf_op | source)
XLA Modules:
  0.0 1343.9 jit_solution(9891540547282636463)
XLA Ops:
  7.9 1.6 bitcast_select_fusion
  9.6 8.9 collective-permute-start.1
  18.6 5.1 collective-permute-start.3
  23.7 20.6 %all-gather = bf16[3,1,4096]{2,0,1:T(4,128)(2,1)S(1)} all-gather(bf16[3,1,256]{2,0,1:T(4,128)(2,1)} %param.16), channel_id=2, replica_groups=mesh['tower'=16,'plate'=16] {'plate'}, dimensions={2}, use_global_device_ids=true | all-gather | bytes 26112 | tf_op jit(solution)/shard_map/all_gather | solution.py:143
  44.3 0.7 maximum_convert_fusion
  45.0 4.7 all-gather.3.cloned.1.call-done
  50.1 492.6 %while.25 = (s32[]{:T(128)}, f32[16,256,128]{2,1,0:T(8,128)S(1)}, f32[16,3,256]{2,1,0:T(4,128)S(1)}, f32[3,768]{1,0:T(4,128)S(1)}, f32[16,128]{1,0:T(8,128)S(1)}...) while((s32[]{:T(128)}, f32[16,256,128]{2,1,0:T(8,128)S(1)}, ...), condition=%wide.region_8.9_spmd, body=%wide.region_0.8_spmd.sunk | while | flops 118017312 | bytes 6281063 | solution.py:174
  63.4 0.7 dynamic-slice_convert_fusion.3
  64.7 0.6 fusion.73
  80.9 0.7 dynamic-slice_convert_fusion.3
  82.2 0.6 fusion.73
  98.5 0.7 dynamic-slice_convert_fusion.3
  99.8 0.6 fusion.73
  116.1 0.7 dynamic-slice_convert_fusion.3
  133.6 0.7 dynamic-slice_convert_fusion.3
  151.2 0.7 dynamic-slice_convert_fusion.3
  168.8 0.7 dynamic-slice_convert_fusion.3
  186.3 0.7 dynamic-slice_convert_fusion.3
  203.9 0.7 dynamic-slice_convert_fusion.3
  221.5 0.7 dynamic-slice_convert_fusion.3
  239.1 0.7 dynamic-slice_convert_fusion.3
  256.6 0.7 dynamic-slice_convert_fusion.3
  274.1 0.7 dynamic-slice_convert_fusion.3
  291.6 0.7 dynamic-slice_convert_fusion.3
  309.2 0.7 dynamic-slice_convert_fusion.3
  326.8 0.7 dynamic-slice_convert_fusion.3
  344.4 0.7 dynamic-slice_convert_fusion.3
  362.0 0.7 dynamic-slice_convert_fusion.3
  379.6 0.7 dynamic-slice_convert_fusion.3
  397.0 0.7 dynamic-slice_convert_fusion.3
  414.6 0.7 dynamic-slice_convert_fusion.3
  432.2 0.7 dynamic-slice_convert_fusion.3
  449.8 0.7 dynamic-slice_convert_fusion.3
  467.4 0.7 dynamic-slice_convert_fusion.3
  485.0 0.7 dynamic-slice_convert_fusion.3
  502.6 0.7 dynamic-slice_convert_fusion.3
  520.1 0.7 dynamic-slice_convert_fusion.3
  537.8 0.7 dynamic-slice_convert_fusion.3
  539.1 0.6 fusion.73
  543.4 0.7 copy-done
  545.3 567.6 %all-reduce.1 = (f32[16,128]{1,0:T(8,128)S(1)}, f32[]{:T(128)}, f32[128]{0:T(128)S(1)}, f32[128]{0:T(128)S(1)}) all-reduce(f32[16,128]{1,0:T(8,128)S(1)} %get-tuple-element.335, f32[]{:T(128)S(6)} %convert_element_type.74, f32[128]{0:T(128)S(1)} %get-tuple-element.336, ...), channel_id=1, replica_groups=mesh['tower'=16,'plate'=16] {'tower','plate'}, use_global_device_ids=true, to_apply=%region_11.12 | all-reduce | flops 2305 | bytes 18440 | tf_op jit(solution)/shard_map/psum | solution.py:187
  1113.6 2.9 collective-permute-start.4
  1117.8 50.0 %all-reduce = f32[16,3,256]{2,1,0:T(4,128)S(1)} all-reduce(f32[16,3,256]{2,1,0:T(4,128)S(1)} %get-tuple-element.333), channel_id=4, replica_groups=mesh['tower'=16,'plate'=16] {'plate'}, use_global_device_ids=true, to_apply=%region_10.11.clone | all-reduce | flops 12288 | bytes 98304
  1167.8 0.7 fusion.28
  1169.0 104.0 %all-reduce.4.cloned.1.call-done = f32[128,128]{1,0:T(8,128)} async-done(((f32[128,128]{1,0:T(8,128)}), f32[128,128]{1,0:T(8,128)}) %all-reduce.4.cloned.1.call-update) | async-done | bytes 65552 | tf_op jit(solution)/shard_map/psum | solution.py:187
  1273.0 1.5 broadcast_multiply_fusion.2
  1274.5 61.2 %reduce-scatter.2.cloned.1.call-done = f32[1,256,128]{2,1,0:T(8,128)} async-done(((f32[16,256,128]{2,1,0:T(8,128)}), f32[1,256,128]{2,1,0:T(8,128)}) %reduce-scatter.2.cloned.1.call-update) | async-done | bytes 131088 | tf_op jit(solution)/shard_map/reduce_scatter | solution.py:178
  1335.7 1.7 broadcast_select_fusion
  (857 shorter events, 160.3 us)
Async XLA Ops:
  7.2 42.8 %copy-start.3 = (s32[1,1,56]{2,1,0:T(1,128)S(1)}, s32[1,1,56]{2,1,0:T(1,128)}, u32[]{:S(2)}) copy-start(s32[1,1,56]{2,1,0:T(1,128)} %param.25) | copy-start | bytes 676
  7.2 42.8 %copy-start.6 = (s32[1,1,56]{2,1,0:T(1,128)S(1)}, s32[1,1,56]{2,1,0:T(1,128)}, u32[]{:S(2)}) copy-start(s32[1,1,56]{2,1,0:T(1,128)} %param.24) | copy-start | bytes 676
  7.2 42.8 %copy-start.7 = (s32[1,1,56]{2,1,0:T(1,128)S(1)}, s32[1,1,56]{2,1,0:T(1,128)}, u32[]{:S(2)}) copy-start(s32[1,1,56]{2,1,0:T(1,128)} %param.23) | copy-start | bytes 676
  7.2 42.8 %copy-start.8 = (f32[128]{0:T(128)S(1)}, f32[128]{0:T(128)}, u32[]{:S(2)}) copy-start(f32[128]{0:T(128)} %param.20) | copy-start | bytes 1540
  7.2 42.8 %copy-start.5 = (bf16[128,128]{1,0:T(8,128)(2,1)S(1)}, bf16[128,128]{1,0:T(8,128)(2,1)}, u32[]{:S(2)}) copy-start(bf16[128,128]{1,0:T(8,128)(2,1)} %param.19) | copy-start | bytes 98308
  7.2 42.8 %copy-start.4 = (f32[128]{0:T(128)S(1)}, f32[128]{0:T(128)}, u32[]{:S(2)}) copy-start(f32[128]{0:T(128)} %param.18) | copy-start | bytes 1540
  7.2 42.8 %copy-start.2 = (bf16[16,128]{1,0:T(8,128)(2,1)S(1)}, bf16[16,128]{1,0:T(8,128)(2,1)}, u32[]{:S(2)}) copy-start(bf16[16,128]{1,0:T(8,128)(2,1)} %param.17) | copy-start | bytes 12292
  7.2 42.5 %all-gather.3.cloned.1.call-start = ((), (), s32[]{:S(2)}) async-start(), calls=%async_computation.1 | async-start | bytes 1114112 | tf_op jit(solution)/shard_map/all_gather | solution.py:142
  9.6 1263.4 %all-reduce.4.cloned.1.call-start = ((), (), s32[]{:S(2)}) async-start(), calls=%async_computation.3 | async-start | bytes 131072 | tf_op jit(solution)/shard_map/psum | solution.py:187
  9.6 34.7 %collective-permute-start.1 = (bf16[3,256]{1,0:T(4,128)(2,1)}, bf16[3,256]{1,0:T(4,128)(2,1)S(1)}, u32[]{:S(2)}, u32[]{:S(2)}) collective-permute-start(bf16[3,256]{1,0:T(4,128)(2,1)} %bitcast.114), channel_id=1, source_target_pairs={{16,0},{32,16},{48,32},{64,48},{80,64},{96,80},{112,96},{128,112},... | collective-permute-start | bytes 4616 | tf_op jit(solution)/shard_map/ppermute | solution.py:22
  18.6 25.7 %collective-permute-start = (bf16[3,256]{1,0:T(4,128)(2,1)}, bf16[3,256]{1,0:T(4,128)(2,1)S(1)}, u32[]{:S(2)}, u32[]{:S(2)}) collective-permute-start(bf16[3,256]{1,0:T(4,128)(2,1)} %bitcast.115), channel_id=1, source_target_pairs={{240,0},{0,16},{16,32},{32,48},{48,64},{64,80},{80,96},{96,112},{1... | collective-permute-start | bytes 4616 | tf_op jit(solution)/shard_map/ppermute | solution.py:22
  18.6 26.4 %collective-permute-start.3 = (bf16[256,128]{1,0:T(8,128)(2,1)S(1)}, bf16[256,128]{1,0:T(8,128)(2,1)S(1)}, u32[]{:S(2)}, u32[]{:S(2)}) collective-permute-start(bf16[256,128]{1,0:T(8,128)(2,1)S(1)} %get-tuple-element.416), channel_id=1, source_target_pairs={{16,0},{32,16},{48,32},{64,48},{80,64},{96,80},{112,96},{128,112},... | collective-permute-start | bytes 196616 | tf_op jit(solution)/shard_map/ppermute | solution.py:22
  23.6 21.4 %collective-permute-start.2 = (bf16[256,128]{1,0:T(8,128)(2,1)S(1)}, bf16[256,128]{1,0:T(8,128)(2,1)S(1)}, u32[]{:S(2)}, u32[]{:S(2)}) collective-permute-start(bf16[256,128]{1,0:T(8,128)(2,1)S(1)} %get-tuple-element.416), channel_id=1, source_target_pairs={{240,0},{0,16},{16,32},{32,48},{48,64},{64,80},{80,96},{96,112},{1... | collective-permute-start | bytes 196616 | tf_op jit(solution)/shard_map/ppermute | solution.py:22
  542.7 0.6 copy-start.1
  542.7 1.3 copy-start
  542.7 2.0 copy-start.9
  543.4 792.4 %reduce-scatter.2.cloned.1.call-start = ((), (), s32[]{:S(2)}) async-start(), calls=%async_computation.2 | async-start | bytes 2228224 | tf_op jit(solution)/shard_map/reduce_scatter | solution.py:178
  1113.6 54.2 %collective-permute-start.4 = (f32[3,256]{1,0:T(4,128)S(1)}, f32[3,256]{1,0:T(4,128)S(1)}, u32[]{:S(2)}, u32[]{:S(2)}) collective-permute-start(f32[3,256]{1,0:T(4,128)S(1)} %get-tuple-element.413), channel_id=1, source_target_pairs={{16,0},{32,16},{48,32},{64,48},{80,64},{96,80},{112,96},{128,112},... | collective-permute-start | bytes 9224 | tf_op jit(solution)/shard_map/ppermute | solution.py:22
  1116.6 51.2 %collective-permute-start.5 = (f32[3,256]{1,0:T(4,128)S(1)}, f32[3,256]{1,0:T(4,128)S(1)}, u32[]{:S(2)}, u32[]{:S(2)}) collective-permute-start(f32[3,256]{1,0:T(4,128)S(1)} %get-tuple-element.414), channel_id=1, source_target_pairs={{240,0},{0,16},{16,32},{32,48},{48,64},{64,80},{80,96},{96,112},{1... | collective-permute-start | bytes 9224 | tf_op jit(solution)/shard_map/ppermute | solution.py:22
Sparse Core Ops, SparseCore 0:
  10.5 39.1 all-gather.2
  543.5 729.4 all-reduce.3
  1275.5 60.1 reduce-scatter.1
where the time goes:
time: 1360 us; the launch traced here: 1340 us
  blocking collectives  638 us (47%)
  loops' own time  313 us (23%)
  waiting for transfers between devices  170 us (12%)
  other arithmetic  75.1 us (6%)
  matrix products  61.3 us (5%)
  local copies, waits for them, and re-layouts  52.8 us (4%)
  starting transfers between devices  17.2 us (1%)
  between operations  16 us (1%)
    psum x1, blocking collectives, local(): lax.psum((acc_weights[0], acc_weights[1], acc_weights[2], acc_weights[3],...  568 us
    another operation x1, loops' own time, local(): lax.fori_loop(0, tile_counts[0, 0], visit_listed, initial)  313 us
    psum x1, waiting for transfers between devices, local(): lax.psum((acc_weights[0], acc_weights[1], acc_weights[2], acc_weights[3],...  104 us
    reduce_scatter x1, waiting for transfers between devices, local(): lax.psum_scatter(acc_dh, 'plate', scatter_dimension=0, tiled=True)  61.2 us
    unnamed x1, blocking collectives  50 us
  transfers between devices with their start and end apart: 9, of which 3 were waited for; matrix products, arithmetic and copies ran while one was open for 0% of the time, Pallas kernels for 0%

commit v1 on v0

v1 whole, which is shorter than its diff:
```python
import math

import jax
import jax.numpy as jnp
from jax import lax
from jax.experimental import pallas as pl
from jax.experimental.pallas import tpu as pltpu

F = 128
TILE = 32
PAIRS = TILE * TILE
MAXT = 56
ROWS = 64
TOWER = 24
PLATE = 128
NRBF = 16
cutoff = 3.0
soften = 0.01
sharp = 10.0
f32 = jnp.float32
bf16 = jnp.bfloat16

NN = (((1,), (0,)), ((), ()))
NT = (((1,), (1,)), ((), ()))
TN = (((0,), (0,)), ((), ()))


def dot(a, b, dims=NN):
    return lax.dot_general(a, b, dims, preferred_element_type=f32)


def iota(shape, axis):
    return lax.broadcasted_iota(jnp.int32, shape, axis)


def split(x):
    hi = x.astype(bf16)
    return hi, (x - hi.astype(f32)).astype(bf16)


def pairs_kernel(
    cnt_s, u_s, v_s,
    adj_ref, feat_ref, tpos_ref, ppos_ref, col_ref, row_ref,
    w1_ref, wr_ref, nwft_ref, hwf_ref,
    gf_ref, gs_ref, gr_ref, gw_ref,
    disp_ref, dist_ref, env_ref, tan_ref, dd_ref, rep_ref,
    *, chunk,
):
    count = cnt_s[0]
    rep = (iota((TILE, PAIRS), 1) // TILE == iota((TILE, PAIRS), 0)).astype(bf16)
    til = (iota((TILE, PAIRS), 1) % TILE == iota((TILE, PAIRS), 0)).astype(bf16)
    rep_ref[...] = rep
    ucol = col_ref[:, 0:1]
    vcol = col_ref[:, 1:2]
    ccol = col_ref[:, 2:3]
    pick_u = (ucol == iota((ROWS, TOWER), 1)).astype(bf16)
    pick_v = (vcol == iota((ROWS, PLATE), 1)).astype(bf16)
    shifts = (ccol // 3 - 1, ccol % 3 - 1, ucol // 8 - 1)
    square = jnp.zeros((ROWS, PAIRS), f32)
    for d in range(3):
        recv = dot(pick_u, tpos_ref[d]).astype(bf16)
        send = dot(pick_v, ppos_ref[d]).astype(bf16)
        disp = dot(recv, rep) - dot(send, til) + shifts[d].astype(f32)
        disp_ref[d] = disp
        square = square + disp * disp
    dist = jnp.sqrt(square + soften)
    dist_ref[...] = dist
    theta = dist * (math.pi / (2 * cutoff))
    inside = (dist < cutoff) & (iota((ROWS, PAIRS), 0) < count)
    cosine = jnp.maximum(jnp.cos(theta), 1e-6)
    env_ref[...] = jnp.where(inside, cosine * cosine, 0.0)
    tan_ref[...] = jnp.where(inside, (-math.pi / cutoff) * jnp.sin(theta) / cosine, 0.0)
    dd_ref[...] = jnp.zeros((ROWS, PAIRS), f32)
    gf_ref[...] = jnp.zeros(gf_ref.shape, f32)
    gw_ref[...] = jnp.zeros(gw_ref.shape, f32)

    centres = iota((NRBF, 1), 0).astype(f32) * (cutoff / (NRBF - 1))
    ones = jnp.ones((NRBF, chunk), bf16)
    w1 = w1_ref[...]
    wr = wr_ref[...]
    nwft = nwft_ref[...]
    hwf = hwf_ref[...]
    fold = (iota((TILE, F), 1) % TILE == iota((TILE, F), 0)).astype(bf16)
    one_row = jnp.ones((NRBF, F), bf16)

    def body(e, carry):
        u = u_s[e]
        v = v_s[e]
        adj = jnp.concatenate([adj_ref[u]] * 2, axis=0)
        feat = feat_ref[v].astype(f32)
        feat4 = jnp.concatenate([feat] * 4, axis=0).T
        wide = jnp.concatenate([feat4] * (chunk // F), axis=1)
        acc = jnp.zeros((F, F), f32)
        gw1 = jnp.zeros((F + NRBF, F), f32)
        gw2 = jnp.zeros((2 * NRBF, F), f32)
        for s in range(0, PAIRS, chunk):
            lanes = pl.ds(s, chunk)
            dist_r = dist_ref[pl.ds(e, 1), lanes]
            env_r = env_ref[pl.ds(e, 1), lanes]
            off = dist_r - centres
            basis = jnp.exp(-sharp * off * off)
            inputs = jnp.concatenate([basis.astype(bf16), ones], axis=0)
            half = dot(w1, inputs)
            t = jnp.tanh(half)
            soft_b = jnp.concatenate([jnp.log(1.0 - t).astype(bf16), ones], axis=0)
            env_hi, env_lo = split(env_r)
            member = rep_ref[:, lanes]
            spread = jnp.concatenate([member * env_hi, member * env_lo], axis=0)
            adj_env = dot(adj, spread, TN)
            d_raw_b = (adj_env * wide).astype(bf16)
            filt = dot(nwft, soft_b)
            d_soft = dot(hwf, d_raw_b)
            d_pre_b = (d_soft * (1.0 + t)).astype(bf16)
            y = adj_env * filt
            for q in range(0, chunk, F):
                acc = acc + y[:, q:q + F]
            z_b = (y * wide).astype(bf16)
            zsum = dot(one_row, z_b)[0:1]
            d_basis = dot(wr, d_pre_b)
            d_dist = jnp.sum(d_basis * basis * off, axis=0, keepdims=True) * (-2.0 * sharp)
            dd_ref[pl.ds(e, 1), lanes] = d_dist + tan_ref[pl.ds(e, 1), lanes] * zsum
            gw1 = gw1 + dot(soft_b, d_raw_b, NT)
            gw2 = gw2 + dot(inputs, d_pre_b, NT)
        gf_ref[v] += dot(fold, acc.astype(bf16), NT)
        gw_ref[0:F + NRBF] += gw1
        gw_ref[F + NRBF:F + 3 * NRBF] += gw2
        return carry

    lax.fori_loop(0, count, body, 0)

    radial = dd_ref[...] / dist_ref[...]
    put_u = (row_ref[0:1] == iota((TOWER, ROWS), 0)).astype(bf16)
    put_v = (row_ref[1:2] == iota((PLATE, ROWS), 0)).astype(bf16)
    for d in range(3):
        hi, lo = split(disp_ref[d] * radial)
        recv_hi, recv_lo = split(dot(hi, rep, NT) + dot(lo, rep, NT))
        send_hi, send_lo = split(dot(hi, til, NT) + dot(lo, til, NT))
        gr_ref[d] = dot(put_u, recv_hi) + dot(put_u, recv_lo)
        gs_ref[d] = -(dot(put_v, send_hi) + dot(put_v, send_lo))


def parts_of(x):
    hi = x.astype(bf16)
    rest = x - hi.astype(f32)
    mid = rest.astype(bf16)
    low = (rest - mid.astype(f32)).astype(bf16)
    return [hi, mid, low]


def pairs(count, tower_tiles, plate_tiles, shifts, adj, feat, tpos, ppos, w_rbf, b_rbf, w_filter, b_filter, chunk=256):
    padded = jnp.pad(jnp.stack([tower_tiles, plate_tiles, shifts]), ((0, 0), (0, ROWS - MAXT)))
    zeros = [jnp.zeros((F,), bf16)] * (NRBF - 3)
    w1 = jnp.concatenate([(w_rbf * 0.5).T, jnp.stack(parts_of(b_rbf * 0.5) + zeros, axis=1)], axis=1)
    nwft = jnp.concatenate([-w_filter.T, jnp.stack(parts_of(b_filter) + zeros, axis=1)], axis=1)
    smem = pl.BlockSpec(memory_space=pltpu.SMEM)
    vmem = pl.BlockSpec(memory_space=pltpu.VMEM)
    return pl.pallas_call(
        lambda *refs: pairs_kernel(*refs, chunk=chunk),
        out_shape=(
            jax.ShapeDtypeStruct((PLATE, TILE, F), f32),
            jax.ShapeDtypeStruct((3, PLATE, TILE), f32),
            jax.ShapeDtypeStruct((3, TOWER, TILE), f32),
            jax.ShapeDtypeStruct((F + 3 * NRBF, F), f32),
        ),
        in_specs=[smem] * 3 + [vmem] * 10,
        out_specs=[vmem] * 4,
        scratch_shapes=[
            pltpu.VMEM((3, ROWS, PAIRS), f32),
            pltpu.VMEM((ROWS, PAIRS), f32),
            pltpu.VMEM((ROWS, PAIRS), f32),
            pltpu.VMEM((ROWS, PAIRS), f32),
            pltpu.VMEM((ROWS, PAIRS), f32),
            pltpu.VMEM((TILE, PAIRS), bf16),
        ],
        compiler_params=pltpu.CompilerParams(vmem_limit_bytes=40 << 20),
        name="pairs",
    )(count, tower_tiles, plate_tiles, adj, feat, tpos, ppos, padded.T, padded, w1, w_rbf, nwft, w_filter * jnp.asarray(0.5, bf16))


def shifted(block, axis, distance):
    devices = range(lax.axis_size(axis))
    route = [((i - distance) % len(devices), i) for i in devices]
    return lax.ppermute(block, axis, route)


def local(features, adjoint, positions, w_rbf, b_rbf, w_filter, b_filter, atom_counts, tile_counts, tower_tiles, plate_tiles, image_shifts):
    atoms = features.shape[1]
    live = jnp.arange(atoms, dtype=jnp.int32) < atom_counts[0, 0]
    zero = jnp.zeros((), bf16)
    own_feat = jnp.where(live[:, None], features[0], zero)
    own_adj = jnp.where(live[:, None], adjoint[0], zero)
    own_pos = positions[:, 0, :]
    below = shifted((own_adj, own_pos), "tower", 1)
    above = shifted((own_adj, own_pos), "tower", -1)
    tower_adj = jnp.concatenate([below[0], own_adj, above[0]], axis=0).reshape(TOWER, TILE, F)
    tower_pos = jnp.concatenate([below[1], own_pos, above[1]], axis=1).reshape(3, TOWER, TILE)
    plate_feat = lax.all_gather(own_feat, "plate", axis=0, tiled=True).reshape(PLATE, TILE, F)
    plate_pos = lax.all_gather(own_pos, "plate", axis=1, tiled=True).reshape(3, PLATE, TILE)
    gf, gs, gr, gw = pairs(
        tile_counts[0], tower_tiles[0, 0], plate_tiles[0, 0], image_shifts[0, 0],
        tower_adj, plate_feat, tower_pos, plate_pos, w_rbf, b_rbf, w_filter, b_filter,
    )
    home = lax.psum_scatter(gf.reshape(16, atoms, F), "plate", scatter_dimension=0, tiled=True)[0]
    home_pos = lax.psum_scatter(gs.reshape(3, 16, atoms), "plate", scatter_dimension=1, tiled=True)[:, 0]
    gr = gr.reshape(3, 3 * atoms)
    back_down = shifted(gr[:, :atoms], "tower", -1)
    back_up = shifted(gr[:, 2 * atoms:], "tower", 1)
    total_pos = home_pos + gr[:, atoms:2 * atoms] + back_down + back_up
    summed, tiles = lax.psum((gw, tile_counts[0, 0].astype(f32)), ("tower", "plate"))
    scale = lax.rsqrt(tiles * (TILE * TILE))
    return (
        jnp.where(live[:, None], home, 0.0)[None],
        total_pos[:, None, :],
        summed[F + NRBF:F + 2 * NRBF] * scale,
        summed[F + 2 * NRBF] * scale,
        summed[0:F] * -scale,
        summed[F] * scale,
    )


def solution(mesh):
    from jax.sharding import PartitionSpec as P
    brick = P("tower", "plate", None)
    one = P("tower", "plate")
    return jax.shard_map(
        local, mesh=mesh,
        in_specs=(brick, brick, P(None, "tower", "plate"), P(), P(), P(), P(), one, one, brick, brick, brick),
        out_specs=(brick, P(None, "tower", "plate"), P(), P(), P(), P()),
        check_vma=False,
    )
```

time: 1360 us -> 462 us (0.34)
  blocking collectives: 638 us -> 146 us
  loops' own time: 313 us -> 0 us
  Pallas kernels: 0 us -> 96.7 us
  other arithmetic: 75.1 us -> 10.8 us
  matrix products: 61.3 us -> 0 us
  local copies, waits for them, and re-layouts: 52.8 us -> 6.5 us
    psum x1, blocking collectives: 568 us -> 74.9 us  [local(): lax.psum((gw, tile_counts[0, 0].astype(f32)), ('tower', 'plate'))]
    another operation x1 -> x0, loops' own time: 313 us -> none  [local(): lax.fori_loop(0, tile_counts[0, 0], visit_listed, initial)]
    pallas_call x0 -> x1, Pallas kernels: none -> 96.7 us  [pairs(): pl.pallas_call(lambda *refs: pairs_kernel(*refs, chunk=chunk), out_shape=...]
    dot_general x168 -> x0, matrix products: 61.3 us -> none  [the longest x28 17 us: pair_tile(): jnp.dot(softed, w_filter, preferred_element_type=jnp.float32) + b_filter]
    dynamic_slice x56 -> x0, local copies, waits for them, and re-layouts: 32.8 us -> none  [the longest x28 16.4 us: visit_listed(): tower_tile = tower_tiles[0, 0, entry]]
    convert_element_type x30 -> x0, other arithmetic: 20.6 us -> none  [the longest x28 19.9 us: pair_tile(): adj_wide = adj_rows.astype(jnp.float32)]
    rem x28 -> x0, other arithmetic: 16.7 us -> none  [shift_vector(): shift_code // 3 - 1]
  transfers between devices with their start and end apart: 9 -> 9, of which waited for: 3 -> 2; matrix products, arithmetic and copies ran while one was open for 0% -> 3% of each run, Pallas kernels for 0% -> 0%
where the time goes in v1:
time: 462 us; the launch traced here: 459 us
  waiting for transfers between devices  166 us (36%)
  blocking collectives  146 us (32%)
  Pallas kernels  96.7 us (21%)
  starting transfers between devices  17.3 us (4%)
  between operations  16 us (3%)
  other arithmetic  10.8 us (2%)
  local copies, waits for them, and re-layouts  6.5 us (1%)
    psum x1, waiting for transfers between devices, local(): lax.psum((gw, tile_counts[0, 0].astype(f32)), ('tower', 'plate'))  107 us
    pallas_call x1, Pallas kernels, pairs(): pl.pallas_call(lambda *refs: pairs_kernel(*refs, chunk=chunk), out_shape=...  96.7 us
    psum x1, blocking collectives, local(): lax.psum((gw, tile_counts[0, 0].astype(f32)), ('tower', 'plate'))  74.9 us
    reduce_scatter x1, waiting for transfers between devices, local(): lax.psum_scatter(gf.reshape(16, atoms, F), 'plate', scatter_dimension=0,...  58.4 us
    unnamed x1, blocking collectives  50 us
    all_gather x1, blocking collectives, local(): lax.all_gather(own_pos, 'plate', axis=1, tiled=True).reshape(3, PLATE, TILE)  20.7 us
    ppermute x6, starting transfers between devices, shifted(): return lax.ppermute(block, axis, route)  17.2 us
  transfers between devices with their start and end apart: 9, of which 2 were waited for; matrix products, arithmetic and copies ran while one was open for 3% of the time, Pallas kernels for 0%

profile of v1, /device:TPU:1, one launch (start us, length us, event | category | flops | bytes accessed | tf_op | source)
XLA Modules:
  0.0 459.0 jit_solution(5004596169243318614)
XLA Ops:
  7.2 0.0 all-gather.3.cloned.1.call-start
  7.9 1.6 bitcast_select_fusion
  9.5 0.0 all-reduce.4.cloned.1.call-start
  9.6 3.7 collective-permute-start
  13.2 5.4 %collective-permute-start.1 = (bf16[256,128]{1,0:T(8,128)(2,1)S(1)}, bf16[256,128]{1,0:T(8,128)(2,1)S(1)}, u32[]{:S(2)}, u32[]{:S(2)}) collective-permute-start(bf16[256,128]{1,0:T(8,128)(2,1)S(1)} %get-tuple-element.51), channel_id=1, source_target_pairs={{16,0},{32,16},{48,32},{64,48},{80,64},{96,80},{112,96},{128,112},... | collective-permute-start | bytes 196616 | tf_op jit(solution)/shard_map/ppermute | solution.py:183
  18.6 5.1 %collective-permute-start.3 = (bf16[3,256]{1,0:T(4,128)(2,1)}, bf16[3,256]{1,0:T(4,128)(2,1)S(1)}, u32[]{:S(2)}, u32[]{:S(2)}) collective-permute-start(bf16[3,256]{1,0:T(4,128)(2,1)} %bitcast.58), channel_id=1, source_target_pairs={{16,0},{32,16},{48,32},{64,48},{80,64},{96,80},{112,96},{128,112},... | collective-permute-start | bytes 4616 | tf_op jit(solution)/shard_map/ppermute | solution.py:183
  23.7 0.9 copy.65
  24.6 0.7 pad_add_fusion
  25.3 0.7 convert_bitcast_fusion
  26.0 0.7 convert_bitcast_fusion.3
  26.7 0.7 broadcast_multiply_fusion.1
  27.4 0.8 broadcast_multiply_fusion.refs_12_
  28.1 20.7 %all-gather = bf16[3,1,4096]{2,0,1:T(4,128)(2,1)S(1)} all-gather(bf16[3,1,256]{2,0,1:T(4,128)(2,1)} %param.14), channel_id=2, replica_groups=mesh['tower'=16,'plate'=16] {'plate'}, dimensions={2}, use_global_device_ids=true | all-gather | bytes 26112 | tf_op jit(solution)/shard_map/all_gather | solution.py:198
  48.8 0.8 concatenate.21
  49.6 0.1 copy.66
  49.7 0.1 copy.67
  49.9 0.1 copy.68
  50.0 0.1 copy.62
  50.2 0.1 copy.63
  50.3 0.1 copy.64
  50.4 0.1 copy.61
  50.6 0.1 copy.69.refs_7_
  51.3 0.1 reshape.53.refs_6_
  51.5 0.1 concatenate.25.refs_11_
  51.6 0.1 concatenate.24.refs_9_
  51.8 0.1 concatenate.20
  51.9 0.1 concatenate.22
  52.0 0.0 all-gather.3.cloned.1.call-done
  52.1 1.2 copy-done
  53.3 96.7 %pairs.1 = (f32[128,32,128]{2,1,0:T(8,128)}, f32[3,128,32]{2,1,0:T(8,128)S(1)}, f32[3,24,32]{2,1,0:T(8,128)S(1)}, f32[176,128]{1,0:T(8,128)}) custom-call(s32[1]{0:T(128)} %bitcast.49.refs_0_, s32[56]{0:T(128)S(1)} %bitcast.53, s32[56]{0:T(128)S(1)} %bitcast.55, bf16[24,32,128]{2,1,0:T(8,128)(2,1)S(1)} %bitcast.51, bf16[128,32,128]{2,1,0:T(8,128)(2,1)S(1)} %bitcast.50, ...), custom_call_target="tpu_custom_call" | custom-call | tf_op jit(solution)/shard_map/pairs/pallas_call | solution.py:157
  150.0 0.0 all-reduce.4.cloned.1.call-update
  150.1 0.0 reduce-scatter.3.cloned.1.call-start
  150.1 0.7 reduce-scatter.3.cloned.1.call-update
  150.8 74.9 %psum.15 = f32[]{:T(128)} all-reduce(f32[]{:T(128)} %bitcast.26), channel_id=1, replica_groups=mesh['tower'=16,'plate'=16] {'tower','plate'}, use_global_device_ids=true, to_apply=%region_3.4 | all-reduce | flops 1 | bytes 8 | tf_op jit(solution)/shard_map/psum | solution.py:209
  226.4 0.6 dynamic-slice
  227.0 0.1 reshape.56
  227.1 1.2 collective-permute-start.4
  228.3 1.9 collective-permute-start.5
  230.2 0.1 reshape.55
  230.3 50.0 %all-reduce.1 = f32[3,16,256]{2,1,0:T(8,128)S(1)} all-reduce(f32[3,16,256]{2,1,0:T(8,128)S(1)} %reshape.55), channel_id=4, replica_groups=mesh['tower'=16,'plate'=16] {'plate'}, use_global_device_ids=true, to_apply=%region_1.2.clone | all-reduce | flops 12288 | bytes 98304
  280.3 0.7 constant_dynamic-slice_fusion
  281.0 0.6 copy.70
  281.6 106.9 %all-reduce.4.cloned.1.call-done = f32[176,128]{1,0:T(8,128)} async-done(((f32[176,128]{1,0:T(8,128)}), f32[176,128]{1,0:T(8,128)}) %all-reduce.4.cloned.1.call-update) | async-done | bytes 90128 | tf_op jit(solution)/shard_map/psum | solution.py:209
  388.5 1.2 fusion.3
  389.7 1.3 slice_multiply_fusion.1
  391.0 1.5 slice_multiply_fusion
  392.4 58.4 %reduce-scatter.3.cloned.1.call-done = f32[1,256,128]{2,1,0:T(8,128)} async-done(((f32[16,256,128]{2,1,0:T(8,128)}), f32[1,256,128]{2,1,0:T(8,128)}) %reduce-scatter.3.cloned.1.call-update) | async-done | bytes 131088 | tf_op jit(solution)/shard_map/reduce_scatter | solution.py:203
  450.9 1.7 broadcast_select_fusion
  (27 shorter events, 0.1 us)
Async XLA Ops:
  7.2 44.9 %copy-start.2 = (s32[1,1,56]{2,1,0:T(1,128)S(1)}, s32[1,1,56]{2,1,0:T(1,128)}, u32[]{:S(2)}) copy-start(s32[1,1,56]{2,1,0:T(1,128)} %param.21) | copy-start | bytes 676
  7.2 44.9 %copy-start.3 = (s32[1,1,56]{2,1,0:T(1,128)S(1)}, s32[1,1,56]{2,1,0:T(1,128)}, u32[]{:S(2)}) copy-start(s32[1,1,56]{2,1,0:T(1,128)} %param.22) | copy-start | bytes 676
  7.2 44.9 %copy-start.1 = (bf16[16,128]{1,0:T(8,128)(2,1)S(1)}, bf16[16,128]{1,0:T(8,128)(2,1)}, u32[]{:S(2)}) copy-start(bf16[16,128]{1,0:T(8,128)(2,1)} %refs_10_.1) | copy-start | bytes 12292
  7.2 44.8 %all-gather.3.cloned.1.call-start = ((), (), s32[]{:S(2)}) async-start(), calls=%async_computation.1 | async-start | bytes 1114112 | tf_op jit(solution)/shard_map/all_gather | solution.py:197
  9.5 378.9 %all-reduce.4.cloned.1.call-start = ((), (), s32[]{:S(2)}) async-start(), calls=%async_computation.3 | async-start | bytes 180224 | tf_op jit(solution)/shard_map/psum | solution.py:209
  9.6 42.4 %collective-permute-start = (bf16[256,128]{1,0:T(8,128)(2,1)S(1)}, bf16[256,128]{1,0:T(8,128)(2,1)S(1)}, u32[]{:S(2)}, u32[]{:S(2)}) collective-permute-start(bf16[256,128]{1,0:T(8,128)(2,1)S(1)} %get-tuple-element.51), channel_id=1, source_target_pairs={{240,0},{0,16},{16,32},{32,48},{48,64},{64,80},{80,96},{96,112},{1... | collective-permute-start | bytes 196616 | tf_op jit(solution)/shard_map/ppermute | solution.py:183
  13.2 38.8 %collective-permute-start.1 = (bf16[256,128]{1,0:T(8,128)(2,1)S(1)}, bf16[256,128]{1,0:T(8,128)(2,1)S(1)}, u32[]{:S(2)}, u32[]{:S(2)}) collective-permute-start(bf16[256,128]{1,0:T(8,128)(2,1)S(1)} %get-tuple-element.51), channel_id=1, source_target_pairs={{16,0},{32,16},{48,32},{64,48},{80,64},{96,80},{112,96},{128,112},... | collective-permute-start | bytes 196616 | tf_op jit(solution)/shard_map/ppermute | solution.py:183
  18.6 33.2 %collective-permute-start.2 = (bf16[3,256]{1,0:T(4,128)(2,1)}, bf16[3,256]{1,0:T(4,128)(2,1)S(1)}, u32[]{:S(2)}, u32[]{:S(2)}) collective-permute-start(bf16[3,256]{1,0:T(4,128)(2,1)} %bitcast.57), channel_id=1, source_target_pairs={{240,0},{0,16},{16,32},{32,48},{48,64},{64,80},{80,96},{96,112},{1... | collective-permute-start | bytes 4616 | tf_op jit(solution)/shard_map/ppermute | solution.py:183
  18.6 33.3 %collective-permute-start.3 = (bf16[3,256]{1,0:T(4,128)(2,1)}, bf16[3,256]{1,0:T(4,128)(2,1)S(1)}, u32[]{:S(2)}, u32[]{:S(2)}) collective-permute-start(bf16[3,256]{1,0:T(4,128)(2,1)} %bitcast.58), channel_id=1, source_target_pairs={{16,0},{32,16},{48,32},{64,48},{80,64},{96,80},{112,96},{128,112},... | collective-permute-start | bytes 4616 | tf_op jit(solution)/shard_map/ppermute | solution.py:183
  52.0 174.5 %copy-start.4 = (u32[256]{0:T(256)S(1)}, u32[256]{0:T(256)}, u32[]{:S(2)}) copy-start(u32[256]{0:T(256)} %constant.28) | copy-start | bytes 3076
  52.1 1.2 copy-start
  150.1 300.8 %reduce-scatter.3.cloned.1.call-start = ((), (), s32[]{:S(2)}) async-start(), calls=%async_computation.2 | async-start | bytes 2228224 | tf_op jit(solution)/shard_map/reduce_scatter | solution.py:203
  227.1 53.8 %collective-permute-start.4 = (f32[3,256]{1,0:T(4,128)S(1)}, f32[3,256]{1,0:T(4,128)S(1)}, u32[]{:S(2)}, u32[]{:S(2)}) collective-permute-start(f32[3,256]{1,0:T(4,128)S(1)} %get-tuple-element.40), channel_id=1, source_target_pairs={{16,0},{32,16},{48,32},{64,48},{80,64},{96,80},{112,96},{128,112},... | collective-permute-start | bytes 9224 | tf_op jit(solution)/shard_map/ppermute | solution.py:183
  228.3 52.7 %collective-permute-start.5 = (f32[3,256]{1,0:T(4,128)S(1)}, f32[3,256]{1,0:T(4,128)S(1)}, u32[]{:S(2)}, u32[]{:S(2)}) collective-permute-start(f32[3,256]{1,0:T(4,128)S(1)} %get-tuple-element.41), channel_id=1, source_target_pairs={{240,0},{0,16},{16,32},{32,48},{48,64},{64,80},{80,96},{96,112},{1... | collective-permute-start | bytes 9224 | tf_op jit(solution)/shard_map/ppermute | solution.py:183
Sparse Core Ops, SparseCore 0:
  10.5 39.1 all-gather.2
  150.2 238.2 all-reduce.3
  391.0 59.8 reduce-scatter.2

commit v2 on v1

v2 whole, which is shorter than its diff:
```python
import math

import jax
import jax.numpy as jnp
from jax import lax
from jax.experimental import pallas as pl
from jax.experimental.pallas import tpu as pltpu

F = 128
TILE = 32
PAIRS = TILE * TILE
MAXT = 56
ATOMS = 256
PACK = ATOMS + 32
BRICKS = 16
WROWS = 16
ROWS = 64
TOWER = 24
PLATE = 128
NRBF = 16
cutoff = 3.0
soften = 0.01
sharp = 10.0
f32 = jnp.float32
bf16 = jnp.bfloat16

NN = (((1,), (0,)), ((), ()))
NT = (((1,), (1,)), ((), ()))
TN = (((0,), (0,)), ((), ()))


def dot(a, b, dims=NN):
    return lax.dot_general(a, b, dims, preferred_element_type=f32)


def iota(shape, axis):
    return lax.broadcasted_iota(jnp.int32, shape, axis)


def split(x):
    hi = x.astype(bf16)
    return hi, (x - hi.astype(f32)).astype(bf16)


def pairs_kernel(
    cnt_s, u_s, v_s,
    tower_ref, plate_ref, col_ref, row_ref,
    w1_ref, wr_ref, nwft_ref, hwf_ref,
    pack_ref, tg_ref, gw_ref,
    disp_ref, dist_ref, env_ref, tan_ref, dd_ref, rep_ref, gf_ref,
    *, chunk,
):
    count = cnt_s[0]
    rep = (iota((TILE, PAIRS), 1) // TILE == iota((TILE, PAIRS), 0)).astype(bf16)
    rep_ref[...] = rep
    rep4 = (iota((F, PAIRS), 1) // TILE == iota((F, PAIRS), 0) % TILE).astype(bf16)
    til4 = (iota((F, PAIRS), 1) % TILE == iota((F, PAIRS), 0) % TILE).astype(bf16)
    ucol = col_ref[:, 0:1]
    vcol = col_ref[:, 1:2]
    ccol = col_ref[:, 2:3]
    group = iota((ROWS, F), 1) // TILE
    in_low_u, in_up_u = group == ucol % 8, group + 4 == ucol % 8
    in_low_v, in_up_v = group == vcol % 8, group + 4 == vcol % 8
    t_low = tower_ref[:, ATOMS:ATOMS + 16, :].reshape(48, F)
    t_up = tower_ref[:, ATOMS + 16:ATOMS + 32, :].reshape(48, F)
    p_low = plate_ref[:, ATOMS:ATOMS + 16, :].reshape(256, F)
    p_up = plate_ref[:, ATOMS + 16:ATOMS + 32, :].reshape(256, F)
    shifts = (ccol // 3 - 1, ccol % 3 - 1, ucol // 8 - 1)
    square = jnp.zeros((ROWS, PAIRS), f32)
    for d in range(3):
        pick_u = (ucol // 8 * 16 + d == iota((ROWS, 48), 1)).astype(bf16)
        pick_v = (vcol // 8 * 16 + d == iota((ROWS, 256), 1)).astype(bf16)
        recv = jnp.where(in_low_u, dot(pick_u, t_low), 0.0) + jnp.where(in_up_u, dot(pick_u, t_up), 0.0)
        send = jnp.where(in_low_v, dot(pick_v, p_low), 0.0) + jnp.where(in_up_v, dot(pick_v, p_up), 0.0)
        disp = dot(recv.astype(bf16), rep4) - dot(send.astype(bf16), til4) + shifts[d].astype(f32)
        disp_ref[d] = disp
        square = square + disp * disp
    dist = jnp.sqrt(square + soften)
    dist_ref[...] = dist
    theta = dist * (math.pi / (2 * cutoff))
    inside = (dist < cutoff) & (iota((ROWS, PAIRS), 0) < count)
    cosine = jnp.maximum(jnp.cos(theta), 1e-6)
    env_ref[...] = jnp.where(inside, cosine * cosine, 0.0)
    tan_ref[...] = jnp.where(inside, (-math.pi / cutoff) * jnp.sin(theta) / cosine, 0.0)
    dd_ref[...] = jnp.zeros((ROWS, PAIRS), f32)
    gf_ref[...] = jnp.zeros(gf_ref.shape, f32)
    gw_ref[...] = jnp.zeros(gw_ref.shape, f32)

    centres = iota((NRBF, 1), 0).astype(f32) * (cutoff / (NRBF - 1))
    ones = jnp.ones((NRBF, chunk), bf16)
    w1 = w1_ref[...]
    wr = wr_ref[...]
    nwft = nwft_ref[...]
    hwf = hwf_ref[...]
    fold = (iota((TILE, 2 * F), 1) % TILE == iota((TILE, 2 * F), 0)).astype(bf16)
    one_row = jnp.ones((NRBF, F), bf16)

    def body(e, carry):
        u = u_s[e]
        v = v_s[e]
        adj = tower_ref[u // 8, pl.ds(pl.multiple_of(u % 8 * TILE, TILE), TILE), :]
        adj = jnp.concatenate([adj] * 2, axis=0)
        feat = plate_ref[v // 8, pl.ds(pl.multiple_of(v % 8 * TILE, TILE), TILE), :].astype(f32)
        feat4 = jnp.concatenate([feat] * 4, axis=0).T
        wide = jnp.concatenate([feat4] * (chunk // F), axis=1)
        acc = jnp.zeros((F, F), f32)
        gw1 = jnp.zeros((F + NRBF, F), f32)
        gw2 = jnp.zeros((2 * NRBF, F), f32)
        for s in range(0, PAIRS, chunk):
            lanes = pl.ds(s, chunk)
            dist_r = dist_ref[pl.ds(e, 1), lanes]
            env_r = env_ref[pl.ds(e, 1), lanes]
            off = dist_r - centres
            basis = jnp.exp(-sharp * off * off)
            inputs = jnp.concatenate([basis.astype(bf16), ones], axis=0)
            half = dot(w1, inputs)
            t = jnp.tanh(half)
            soft_b = jnp.concatenate([jnp.log(1.0 - t).astype(bf16), ones], axis=0)
            env_hi, env_lo = split(env_r)
            member = rep_ref[:, lanes]
            spread = jnp.concatenate([member * env_hi, member * env_lo], axis=0)
            adj_env = dot(adj, spread, TN)
            d_raw_b = (adj_env * wide).astype(bf16)
            filt = dot(nwft, soft_b)
            d_soft = dot(hwf, d_raw_b)
            d_pre_b = (d_soft * (1.0 + t)).astype(bf16)
            y = adj_env * filt
            for q in range(0, chunk, F):
                acc = acc + y[:, q:q + F]
            z_b = (y * wide).astype(bf16)
            zsum = dot(one_row, z_b)[0:1]
            d_basis = dot(wr, d_pre_b)
            d_dist = jnp.sum(d_basis * basis * off, axis=0, keepdims=True) * (-2.0 * sharp)
            dd_ref[pl.ds(e, 1), lanes] = d_dist + tan_ref[pl.ds(e, 1), lanes] * zsum
            gw1 = gw1 + dot(soft_b, d_raw_b, NT)
            gw2 = gw2 + dot(inputs, d_pre_b, NT)
        gf_ref[v] += dot(fold, jnp.concatenate(split(acc), axis=1), NT)
        gw_ref[0:9] += gw1.reshape(9, WROWS, F)
        gw_ref[9:11] += gw2.reshape(2, WROWS, F)
        return carry

    lax.fori_loop(0, count, body, 0)

    radial = dd_ref[...] / dist_ref[...]
    rrow = row_ref[0:1]
    srow = row_ref[1:2]
    t_sums = [jnp.zeros((48, F), f32), jnp.zeros((48, F), f32)]
    p_sums = [jnp.zeros((256, F), f32), jnp.zeros((256, F), f32)]
    for d in range(3):
        hi, lo = split(disp_ref[d] * radial)
        recv = dot(hi, rep4, NT) + dot(lo, rep4, NT)
        send = -(dot(hi, til4, NT) + dot(lo, til4, NT))
        put_u = (rrow // 8 * 16 + d == iota((48, ROWS), 0)).astype(bf16)
        put_v = (srow // 8 * 16 + d == iota((256, ROWS), 0)).astype(bf16)
        for k, mask in enumerate((in_low_u, in_up_u)):
            hi, lo = split(jnp.where(mask, recv, 0.0))
            t_sums[k] = t_sums[k] + dot(put_u, hi) + dot(put_u, lo)
        for k, mask in enumerate((in_low_v, in_up_v)):
            hi, lo = split(jnp.where(mask, send, 0.0))
            p_sums[k] = p_sums[k] + dot(put_v, hi) + dot(put_v, lo)
    for k in range(2):
        rows = pl.ds(16 * k, 16)
        tg_ref[:, rows, :] = t_sums[k].reshape(3, 16, F)
        pack_ref[:, pl.ds(ATOMS + 16 * k, 16), :] = p_sums[k].astype(bf16).reshape(BRICKS, 16, F)
    pack_ref[:, 0:ATOMS, :] = gf_ref[...].reshape(BRICKS, ATOMS, F).astype(bf16)
    gw_ref[11] = jnp.full((WROWS, F), count, jnp.int32).astype(f32)


def parts_of(x):
    hi = x.astype(bf16)
    rest = x - hi.astype(f32)
    mid = rest.astype(bf16)
    low = (rest - mid.astype(f32)).astype(bf16)
    return [hi, mid, low]


def pairs(count, tower_tiles, plate_tiles, shifts, tower, plate, w_rbf, b_rbf, w_filter, b_filter, chunk=256):
    padded = jnp.pad(jnp.stack([tower_tiles, plate_tiles, shifts]), ((0, 0), (0, ROWS - MAXT)))
    zeros = [jnp.zeros((F,), bf16)] * (NRBF - 3)
    w1 = jnp.concatenate([(w_rbf * 0.5).T, jnp.stack(parts_of(b_rbf * 0.5) + zeros, axis=1)], axis=1)
    nwft = jnp.concatenate([-w_filter.T, jnp.stack(parts_of(b_filter) + zeros, axis=1)], axis=1)
    smem = pl.BlockSpec(memory_space=pltpu.SMEM)
    vmem = pl.BlockSpec(memory_space=pltpu.VMEM)
    return pl.pallas_call(
        lambda *refs: pairs_kernel(*refs, chunk=chunk),
        out_shape=(
            jax.ShapeDtypeStruct((BRICKS, PACK, F), bf16),
            jax.ShapeDtypeStruct((3, 32, F), f32),
            jax.ShapeDtypeStruct((16, WROWS, F), f32),
        ),
        in_specs=[smem] * 3 + [vmem] * 8,
        out_specs=[vmem] * 3,
        scratch_shapes=[
            pltpu.VMEM((3, ROWS, PAIRS), f32),
            pltpu.VMEM((ROWS, PAIRS), f32),
            pltpu.VMEM((ROWS, PAIRS), f32),
            pltpu.VMEM((ROWS, PAIRS), f32),
            pltpu.VMEM((ROWS, PAIRS), f32),
            pltpu.VMEM((TILE, PAIRS), bf16),
            pltpu.VMEM((PLATE, TILE, F), f32),
        ],
        compiler_params=pltpu.CompilerParams(vmem_limit_bytes=40 << 20),
        name="pairs",
    )(count, tower_tiles, plate_tiles, tower, plate, padded.T, padded, w1, w_rbf, nwft, w_filter * jnp.asarray(0.5, bf16))


def send_to(src, dst, sends, recvs, slot, device):
    copy = pltpu.make_async_remote_copy(
        src_ref=src, dst_ref=dst, send_sem=sends.at[slot], recv_sem=recvs.at[slot],
        device_id=device, device_id_type=pl.DeviceIdType.MESH,
    )
    copy.start()
    return copy


def greet(devices):
    barrier = pltpu.get_barrier_semaphore()
    for device in devices:
        pl.semaphore_signal(barrier, inc=1, device_id=device, device_id_type=pl.DeviceIdType.MESH)
    pl.semaphore_wait(barrier, len(devices))


def gather_kernel(cnt_s, feat_ref, adj_ref, pos_ref, plate_ref, tower_ref, chip_send, chip_recv, mate_send, mate_recv, tower_send, tower_recv):
    t = lax.axis_index("tower")
    p = lax.axis_index("plate")
    q, core = p // 2, p % 2
    mate = (t, q * 2 + 1 - core)
    above = ((t + 1) % 16, p)
    below = ((t + 15) % 16, p)
    chips = [(q + d) % 8 for d in range(8)]
    back = [(q + 8 - d) % 8 for d in range(8)]
    live = iota((ATOMS, F), 0) < cnt_s[0]
    zero = jnp.zeros((13, F), bf16)
    for rows, ref, slot in ((feat_ref, plate_ref, p), (adj_ref, tower_ref, 1)):
        ref[slot, 0:ATOMS, :] = jnp.where(live, rows[...].astype(f32), 0.0).astype(bf16)
        for k in range(2):
            ref[slot, pl.ds(ATOMS + 16 * k, 16), :] = jnp.concatenate([pos_ref[:, k * F:(k + 1) * F].astype(f32), jnp.zeros((13, F), f32)], axis=0).astype(bf16)
    greet([(t, chips[d] * 2 + core) for d in range(1, 8)] + [mate, above, below])
    mine = plate_ref.at[p]
    out = [send_to(mine, mine, chip_send, chip_recv, d, (t, chips[d] * 2 + core)) for d in range(1, 8)]
    out.append(send_to(mine, mine, mate_send, mate_recv, 0, mate))
    up = send_to(tower_ref.at[1], tower_ref.at[0], tower_send, tower_recv, 0, above)
    down = send_to(tower_ref.at[1], tower_ref.at[2], tower_send, tower_recv, 1, below)
    passed = []
    for d in range(1, 8):
        out[d - 1].wait_recv()
        block = plate_ref.at[back[d] * 2 + core]
        passed.append(send_to(block, block, mate_send, mate_recv, d, mate))
    for copy in out:
        copy.wait_send()
    out[7].wait_recv()
    for copy in passed + [up, down]:
        copy.wait()


def gather(count, feat, adj, pos):
    smem = pl.BlockSpec(memory_space=pltpu.SMEM)
    vmem = pl.BlockSpec(memory_space=pltpu.VMEM)
    return pl.pallas_call(
        gather_kernel,
        out_shape=(jax.ShapeDtypeStruct((BRICKS, PACK, F), bf16), jax.ShapeDtypeStruct((3, PACK, F), bf16)),
        in_specs=[smem] + [vmem] * 3,
        out_specs=[vmem] * 2,
        scratch_shapes=[pltpu.SemaphoreType.DMA((8,))] * 4 + [pltpu.SemaphoreType.DMA((2,))] * 2,
        compiler_params=pltpu.CompilerParams(collective_id=0, has_side_effects=True, vmem_limit_bytes=24 << 20),
        name="gather",
    )(count, feat, adj, pos)


def reduce_kernel(
    cnt_s, pack_ref, tg_ref, gw_ref, gf_out, gp_out, wr_out, br_out, wf_out, bf_out,
    mate_buf, send_buf, chip_buf, tower_buf, w1_buf, w2_own, w2_buf, w3_buf,
    mate_send, mate_recv, chip_send, chip_recv, tower_send, tower_recv, w_send, w_recv,
):
    t = lax.axis_index("tower")
    p = lax.axis_index("plate")
    q, core = p // 2, p % 2
    mate = (t, q * 2 + 1 - core)
    chips = [(q + d) % 8 for d in range(8)]
    plate = [(t, (p + d) % 16) for d in range(16)]
    tower = [((t + d) % 16, p) for d in range(16)]
    greet(plate[1:] + tower[1:])
    first = [send_to(gw_ref.at[(p + d) % 16], w1_buf.at[d], w_send.at[0], w_recv.at[0], d, plate[d]) for d in range(1, 16)]
    halves = [send_to(pack_ref.at[chips[d] * 2 + 1 - core], mate_buf.at[d], mate_send, mate_recv, d, mate) for d in (1, 2, 3, 4, 5, 6, 7, 0)]
    up = send_to(tg_ref.at[2], tower_buf.at[0], tower_send, tower_recv, 0, tower[1])
    down = send_to(tg_ref.at[0], tower_buf.at[1], tower_send, tower_recv, 1, tower[15])
    total = gw_ref[p]
    for d in range(1, 16):
        first[d - 1].wait_recv()
        total = total + w1_buf[d]
    w2_own[...] = total
    second = [send_to(w2_own, w2_buf.at[d], w_send.at[1], w_recv.at[1], d, tower[d]) for d in range(1, 16)]
    chip = []
    for d in range(1, 8):
        halves[d - 1].wait_recv()
        send_buf[d] = (pack_ref[chips[d] * 2 + core].astype(f32) + mate_buf[d].astype(f32)).astype(bf16)
        chip.append(send_to(send_buf.at[d], chip_buf.at[d], chip_send, chip_recv, d, (t, chips[d] * 2 + core)))
    for d in range(1, 16):
        second[d - 1].wait_recv()
        total = total + w2_buf[d]
    w3_buf[p] = total
    third = [send_to(w3_buf.at[p], w3_buf.at[p], w_send.at[2], w_recv.at[2], d, plate[d]) for d in range(1, 16)]
    halves[7].wait_recv()
    acc = pack_ref[p].astype(f32) + mate_buf[0].astype(f32)
    for d in range(1, 8):
        chip[d - 1].wait_recv()
        acc = acc + chip_buf[d].astype(f32)
    gf_out[...] = jnp.where(iota((ATOMS, F), 0) < cnt_s[0], acc[0:ATOMS], 0.0)
    up.wait_recv()
    down.wait_recv()
    moved = acc[ATOMS:PACK] + tg_ref[1] + tower_buf[0] + tower_buf[1]
    for k in range(2):
        gp_out[:, k * F:(k + 1) * F] = moved[16 * k:16 * k + 3]
    for d in range(1, 16):
        third[d - 1].wait_recv()
    scale = lax.rsqrt(w3_buf[11][0:1] * (TILE * TILE))
    wf_out[...] = w3_buf[0:8].reshape(F, F) * -scale
    bf_out[...] = w3_buf[8][0:1] * scale
    wr_out[...] = w3_buf[9] * scale
    br_out[...] = w3_buf[10][0:1] * scale
    for copy in first + halves + [up, down] + second + chip + third:
        copy.wait_send()


def reduce(count, pack, tg, gw):
    smem = pl.BlockSpec(memory_space=pltpu.SMEM)
    vmem = pl.BlockSpec(memory_space=pltpu.VMEM)
    weights = pltpu.VMEM((16, WROWS, F), f32)
    dma = pltpu.SemaphoreType.DMA
    return pl.pallas_call(
        reduce_kernel,
        out_shape=(
            jax.ShapeDtypeStruct((ATOMS, F), f32), jax.ShapeDtypeStruct((3, ATOMS), f32), jax.ShapeDtypeStruct((NRBF, F), f32),
            jax.ShapeDtypeStruct((1, F), f32), jax.ShapeDtypeStruct((F, F), f32), jax.ShapeDtypeStruct((1, F), f32),
        ),
        in_specs=[smem] + [vmem] * 3,
        out_specs=[vmem] * 6,
        scratch_shapes=[pltpu.VMEM((8, PACK, F), bf16)] * 3 + [
            pltpu.VMEM((2, 32, F), f32), weights, pltpu.VMEM((WROWS, F), f32), weights, weights,
            dma((8,)), dma((8,)), dma((8,)), dma((8,)), dma((2,)), dma((2,)), dma((3, 16)), dma((3, 16)),
        ],
        compiler_params=pltpu.CompilerParams(collective_id=1, has_side_effects=True, vmem_limit_bytes=24 << 20),
        name="reduce",
    )(count, pack, tg, gw)


def local(features, adjoint, positions, w_rbf, b_rbf, w_filter, b_filter, atom_counts, tile_counts, tower_tiles, plate_tiles, image_shifts):
    plate, tower = gather(atom_counts[0], features[0], adjoint[0], positions[:, 0, :])
    pack, tg, gw = pairs(
        tile_counts[0], tower_tiles[0, 0], plate_tiles[0, 0], image_shifts[0, 0],
        tower, plate, w_rbf, b_rbf, w_filter, b_filter,
    )
    gf, gp, wr, br, wf, bf = reduce(atom_counts[0], pack, tg, gw)
    return gf[None], gp[:, None, :], wr, br[0], wf, bf[0]


def solution(mesh):
    from jax.sharding import PartitionSpec as P
    brick = P("tower", "plate", None)
    one = P("tower", "plate")
    return jax.shard_map(
        local, mesh=mesh,
        in_specs=(brick, brick, P(None, "tower", "plate"), P(), P(), P(), P(), one, one, brick, brick, brick),
        out_specs=(brick, P(None, "tower", "plate"), P(), P(), P(), P()),
        check_vma=False,
    )
```

time: 462 us -> 152 us (0.33)
  waiting for transfers between devices: 166 us -> 0 us
  blocking collectives: 146 us -> 0 us
  Pallas kernels: 96.7 us -> 140 us
  starting transfers between devices: 17.3 us -> 0 us
  between operations: 16 us -> 2.14 us
  other arithmetic: 10.8 us -> 3.56 us
    psum x1 -> x0, waiting for transfers between devices: 107 us -> none  [local(): lax.psum((gw, tile_counts[0, 0].astype(f32)), ('tower', 'plate'))]
    pallas_call x0 -> x2, Pallas kernels: none -> 89.7 us  [the longest x1 68.4 us: reduce(): pl.pallas_call(reduce_kernel, out_shape=(jax.ShapeDtypeStruct((ATOMS, F),...]
    psum x1 -> x0, blocking collectives: 74.9 us -> none  [local(): lax.psum((gw, tile_counts[0, 0].astype(f32)), ('tower', 'plate'))]
    reduce_scatter x1 -> x0, waiting for transfers between devices: 58.4 us -> none  [local(): lax.psum_scatter(gf.reshape(16, atoms, F), 'plate', scatter_dimension=0,...]
    unnamed x1 -> x0, blocking collectives: 50 us -> none
    pallas_call x1, Pallas kernels: 96.7 us -> 50.3 us  [pairs(): pl.pallas_call(lambda *refs: pairs_kernel(*refs, chunk=chunk), out_shape=...]
    all_gather x1 -> x0, blocking collectives: 20.7 us -> none  [local(): lax.all_gather(own_pos, 'plate', axis=1, tiled=True).reshape(3, PLATE, TILE)]
    ppermute x6 -> x0, starting transfers between devices: 17.2 us -> none  [shifted(): return lax.ppermute(block, axis, route)]
  transfers between devices with their start and end apart: 9 -> 0, of which waited for: 2 -> 0; matrix products, arithmetic and copies ran while one was open for 3% -> 0% of each run, Pallas kernels for 0% -> 0%
where the time goes in v2:
time: 152 us; the launch traced here: 151 us
  Pallas kernels  140 us (92%)
  local copies, waits for them, and re-layouts  5.72 us (4%)
  other arithmetic  3.56 us (2%)
  between operations  2.14 us (1%)
    pallas_call x1, Pallas kernels, reduce(): pl.pallas_call(reduce_kernel, out_shape=(jax.ShapeDtypeStruct((ATOMS, F),...  68.4 us
    pallas_call x1, Pallas kernels, pairs(): pl.pallas_call(lambda *refs: pairs_kernel(*refs, chunk=chunk), out_shape=...  50.3 us
    pallas_call x1, Pallas kernels, gather(): pl.pallas_call(gather_kernel, out_shape=(jax.ShapeDtypeStruct((BRICKS, PA...  21.4 us
    unnamed x19, local copies, waits for them, and re-layouts  4.38 us

profile of v2, /device:TPU:1, one launch (start us, length us, event | category | flops | bytes accessed | tf_op | source)
XLA Modules:
  0.0 151.5 jit_solution(155020728275929611)
XLA Ops:
  0.6 0.0 copy-start.4
  0.6 0.0 copy-start.3
  0.7 0.0 copy-start.2
  0.7 0.0 copy-start.5
  0.7 0.0 copy-start.1
  0.7 0.0 copy-start
  2.0 0.7 convert_bitcast_fusion.3
  2.7 0.7 convert_bitcast_fusion
  3.4 0.7 pad_add_fusion
  4.1 0.7 broadcast_multiply_fusion.1
  4.8 0.1 copy.50
  4.9 0.1 copy.57
  5.1 0.1 copy.53
  5.2 0.1 copy.58.refs_5_
  5.3 0.1 copy.56
  5.4 0.1 copy.55
  5.6 0.1 copy.52
  5.7 0.1 copy.51
  5.9 0.1 concatenate.6.refs_7_
  6.1 0.8 broadcast_multiply_fusion.refs_10_
  6.8 0.9 copy.54
  7.7 0.1 concatenate.7.refs_9_
  7.8 0.0 copy-done.5
  7.9 0.0 copy-done.1
  7.9 0.0 copy-done
  7.9 21.4 %gather.1 = (bf16[16,288,128]{2,1,0:T(8,128)(2,1)S(1)}, bf16[3,288,128]{2,1,0:T(8,128)(2,1)S(1)}) custom-call(s32[1]{0:T(128)} %bitcast.31.cnt_s, bf16[256,128]{1,0:T(8,128)(2,1)S(1)} %bitcast.35, bf16[256,128]{1,0:T(8,128)(2,1)S(1)} %bitcast.36, bf16[3,256]{1,0:T(4,128)(2,1)S(1)} %bitcast.42), custom_call_target="tpu_custom_call" | custom-call | tf_op jit(solution)/shard_map/gather/pallas_call | solution.py:259
  29.3 0.0 copy-done.4
  29.3 0.0 copy-done.3
  29.3 0.0 copy-done.2
  29.3 50.3 %pairs.1 = (bf16[16,288,128]{2,1,0:T(8,128)(2,1)S(1)}, f32[3,32,128]{2,1,0:T(8,128)S(1)}, f32[16,16,128]{2,1,0:T(8,128)S(1)}) custom-call(s32[1]{0:T(128)} %bitcast.33.refs_0_, s32[56]{0:T(128)S(1)} %bitcast.39, s32[56]{0:T(128)S(1)} %bitcast.41, bf16[3,288,128]{2,1,0:T(8,128)(2,1)S(1)} %get-tuple-element.17.refs_3_, ...), custom_call_target="tpu_custom_call" | custom-call | tf_op jit(solution)/shard_map/pairs/pallas_call | solution.py:184
  79.6 68.4 %reduce.1 = (f32[256,128]{1,0:T(8,128)S(1)}, f32[3,256]{1,0:T(4,128)S(1)}, f32[16,128]{1,0:T(8,128)S(1)}, f32[1,128]{1,0:T(1,128)S(1)}, f32[128,128]{1,0:T(8,128)S(1)}, /*index=5*/f32[1,128]{1,0:T(1,128)S(1)}) custom-call(s32[1]{0:T(128)} %bitcast.32.cnt_s, bf16[16,288,128]{2,1,0:T(8,128)(2,1)S(1)} %get-tuple-element.19.pack_ref, ...), custom_call_target="tpu_custom_call" | custom-call | tf_op jit(solution)/shard_map/reduce/pallas_call | solution.py:330
  148.0 0.6 copy.59
  148.6 0.7 copy.67
  149.2 0.6 copy.68
  149.8 0.5 copy.69
  150.4 0.6 copy.70
  151.0 0.5 copy.71
  (5 shorter events, 0.0 us)
Async XLA Ops:
  0.6 28.6 %copy-start.4 = (s32[1,1,56]{2,1,0:T(1,128)S(1)}, s32[1,1,56]{2,1,0:T(1,128)}, u32[]{:S(2)}) copy-start(s32[1,1,56]{2,1,0:T(1,128)} %param.22) | copy-start | bytes 676
  0.6 28.6 %copy-start.3 = (s32[1,1,56]{2,1,0:T(1,128)S(1)}, s32[1,1,56]{2,1,0:T(1,128)}, u32[]{:S(2)}) copy-start(s32[1,1,56]{2,1,0:T(1,128)} %param.21) | copy-start | bytes 676
  0.7 28.6 %copy-start.2 = (bf16[16,128]{1,0:T(8,128)(2,1)S(1)}, bf16[16,128]{1,0:T(8,128)(2,1)}, u32[]{:S(2)}) copy-start(bf16[16,128]{1,0:T(8,128)(2,1)} %refs_8_.1) | copy-start | bytes 12292
  0.7 7.2 %copy-start.5 = (bf16[3,1,256]{2,0,1:T(4,128)(2,1)S(1)}, bf16[3,1,256]{2,0,1:T(4,128)(2,1)}, u32[]{:S(2)}) copy-start(bf16[3,1,256]{2,0,1:T(4,128)(2,1)} %param.14) | copy-start | bytes 4612
  0.7 7.2 %copy-start.1 = (bf16[1,256,128]{2,1,0:T(8,128)(2,1)S(1)}, bf16[1,256,128]{2,1,0:T(8,128)(2,1)}, u32[]{:S(2)}) copy-start(bf16[1,256,128]{2,1,0:T(8,128)(2,1)} %param.13) | copy-start | bytes 196612
  0.7 7.2 %copy-start = (bf16[1,256,128]{2,1,0:T(8,128)(2,1)S(1)}, bf16[1,256,128]{2,1,0:T(8,128)(2,1)}, u32[]{:S(2)}) copy-start(bf16[1,256,128]{2,1,0:T(8,128)(2,1)} %param.12) | copy-start | bytes 196612

commit v3 on v2

--- a/solution.py
+++ b/solution.py
@@ -42,34 +42,56 @@
     return hi, (x - hi.astype(f32)).astype(bf16)
 
 
+def sine(x):
+    y = x * x
+    acc = jnp.full_like(x, 1.0 / 6227020800.0)
+    for c in (-1.0 / 39916800.0, 1.0 / 362880.0, -1.0 / 5040.0, 1.0 / 120.0, -1.0 / 6.0, 1.0):
+        acc = acc * y + c
+    return acc * x
+
+
+def three(x):
+    hi = x.astype(bf16).astype(f32)
+    mid = (x - hi).astype(bf16).astype(f32)
+    return [hi, mid, x - hi - mid]
+
+
 def pairs_kernel(
     cnt_s, u_s, v_s,
-    tower_ref, plate_ref, col_ref, row_ref,
-    w1_ref, wr_ref, nwft_ref, hwf_ref,
+    tower_ref, plate_ref, u_ref, v_ref, c_ref,
+    wr_ref, br_ref, wf_ref, bf_ref,
     pack_ref, tg_ref, gw_ref,
-    disp_ref, dist_ref, env_ref, tan_ref, dd_ref, rep_ref, gf_ref,
-    *, chunk,
+    disp_ref, dist_ref, env_ref, tan_ref, dd_ref, rep_ref, gf_ref, list_ref,
+    *, chunk, tiles,
 ):
-    count = cnt_s[0]
-    rep = (iota((TILE, PAIRS), 1) // TILE == iota((TILE, PAIRS), 0)).astype(bf16)
+    count = cnt_s[0, 0]
+    list_ref[...] = jnp.zeros(list_ref.shape, f32)
+    for k, ref in enumerate((u_ref, v_ref, c_ref)):
+        list_ref[k:k + 1, 0:MAXT] = ref[0].astype(f32)
+    lists = list_ref[...]
+    columns = lists.T.astype(jnp.int32)
+    rrow = lists[0:1, 0:ROWS].astype(jnp.int32)
+    srow = lists[1:2, 0:ROWS].astype(jnp.int32)
+    ucol = columns[0:ROWS, 0:1]
+    vcol = columns[0:ROWS, 1:2]
+    ccol = columns[0:ROWS, 2:3]
+    rep = (iota((TILE, PAIRS), 1) >> 5 == iota((TILE, PAIRS), 0)).astype(bf16)
     rep_ref[...] = rep
-    rep4 = (iota((F, PAIRS), 1) // TILE == iota((F, PAIRS), 0) % TILE).astype(bf16)
-    til4 = (iota((F, PAIRS), 1) % TILE == iota((F, PAIRS), 0) % TILE).astype(bf16)
-    ucol = col_ref[:, 0:1]
-    vcol = col_ref[:, 1:2]
-    ccol = col_ref[:, 2:3]
-    group = iota((ROWS, F), 1) // TILE
-    in_low_u, in_up_u = group == ucol % 8, group + 4 == ucol % 8
-    in_low_v, in_up_v = group == vcol % 8, group + 4 == vcol % 8
+    rep4 = (iota((F, PAIRS), 1) >> 5 == (iota((F, PAIRS), 0) & 31)).astype(bf16)
+    til4 = ((iota((F, PAIRS), 1) & 31) == (iota((F, PAIRS), 0) & 31)).astype(bf16)
+    group = iota((ROWS, F), 1) >> 5
+    in_low_u, in_up_u = group == (ucol & 7), group + 4 == (ucol & 7)
+    in_low_v, in_up_v = group == (vcol & 7), group + 4 == (vcol & 7)
     t_low = tower_ref[:, ATOMS:ATOMS + 16, :].reshape(48, F)
     t_up = tower_ref[:, ATOMS + 16:ATOMS + 32, :].reshape(48, F)
     p_low = plate_ref[:, ATOMS:ATOMS + 16, :].reshape(256, F)
     p_up = plate_ref[:, ATOMS + 16:ATOMS + 32, :].reshape(256, F)
-    shifts = (ccol // 3 - 1, ccol % 3 - 1, ucol // 8 - 1)
+    third = (ccol >= 3).astype(jnp.int32) + (ccol >= 6).astype(jnp.int32)
+    shifts = (third - 1, ccol - 3 * third - 1, (ucol >> 3) - 1)
     square = jnp.zeros((ROWS, PAIRS), f32)
     for d in range(3):
-        pick_u = (ucol // 8 * 16 + d == iota((ROWS, 48), 1)).astype(bf16)
-        pick_v = (vcol // 8 * 16 + d == iota((ROWS, 256), 1)).astype(bf16)
+        pick_u = ((ucol >> 3) * 16 + d == iota((ROWS, 48), 1)).astype(bf16)
+        pick_v = ((vcol >> 3) * 16 + d == iota((ROWS, 256), 1)).astype(bf16)
         recv = jnp.where(in_low_u, dot(pick_u, t_low), 0.0) + jnp.where(in_up_u, dot(pick_u, t_up), 0.0)
         send = jnp.where(in_low_v, dot(pick_v, p_low), 0.0) + jnp.where(in_up_v, dot(pick_v, p_up), 0.0)
         disp = dot(recv.astype(bf16), rep4) - dot(send.astype(bf16), til4) + shifts[d].astype(f32)
@@ -77,81 +99,92 @@
         square = square + disp * disp
     dist = jnp.sqrt(square + soften)
     dist_ref[...] = dist
-    theta = dist * (math.pi / (2 * cutoff))
     inside = (dist < cutoff) & (iota((ROWS, PAIRS), 0) < count)
-    cosine = jnp.maximum(jnp.cos(theta), 1e-6)
+    theta = jnp.minimum(dist, cutoff) * (math.pi / (2 * cutoff))
+    cosine = jnp.maximum(sine(math.pi / 2 - theta), 1e-6)
     env_ref[...] = jnp.where(inside, cosine * cosine, 0.0)
-    tan_ref[...] = jnp.where(inside, (-math.pi / cutoff) * jnp.sin(theta) / cosine, 0.0)
+    tan_ref[...] = jnp.where(inside, (-math.pi / cutoff) * sine(theta) / cosine, 0.0)
     dd_ref[...] = jnp.zeros((ROWS, PAIRS), f32)
     gf_ref[...] = jnp.zeros(gf_ref.shape, f32)
     gw_ref[...] = jnp.zeros(gw_ref.shape, f32)
 
     centres = iota((NRBF, 1), 0).astype(f32) * (cutoff / (NRBF - 1))
     ones = jnp.ones((NRBF, chunk), bf16)
-    w1 = w1_ref[...]
     wr = wr_ref[...]
-    nwft = nwft_ref[...]
-    hwf = hwf_ref[...]
-    fold = (iota((TILE, 2 * F), 1) % TILE == iota((TILE, 2 * F), 0)).astype(bf16)
+    zeros = jnp.zeros((NRBF - 3, F), f32)
+    w1 = jnp.concatenate([wr.astype(f32) * 0.5] + three(br_ref[...] * 0.5) + [zeros], axis=0).T.astype(bf16)
+    wf = wf_ref[...].astype(f32)
+    nwft = jnp.concatenate([-wf.T, jnp.concatenate(three(bf_ref[...]) + [zeros], axis=0).T], axis=1).astype(bf16)
+    hwf = (wf * 0.5).astype(bf16)
+    fold = ((iota((TILE, 2 * F), 1) & 31) == iota((TILE, 2 * F), 0)).astype(bf16)
     one_row = jnp.ones((NRBF, F), bf16)
 
-    def body(e, carry):
-        u = u_s[e]
-        v = v_s[e]
-        adj = tower_ref[u // 8, pl.ds(pl.multiple_of(u % 8 * TILE, TILE), TILE), :]
-        adj = jnp.concatenate([adj] * 2, axis=0)
-        feat = plate_ref[v // 8, pl.ds(pl.multiple_of(v % 8 * TILE, TILE), TILE), :].astype(f32)
-        feat4 = jnp.concatenate([feat] * 4, axis=0).T
-        wide = jnp.concatenate([feat4] * (chunk // F), axis=1)
-        acc = jnp.zeros((F, F), f32)
+    def body(step, carry):
+        entries = [step * tiles + k for k in range(tiles)]
+        streams = []
+        for e in entries:
+            u = u_s[0, 0, e]
+            v = v_s[0, 0, e]
+            adj = tower_ref[u >> 3, pl.ds(pl.multiple_of((u & 7) * TILE, TILE), TILE), :]
+            adj = jnp.concatenate([adj] * 2, axis=0)
+            feat = plate_ref[v >> 3, pl.ds(pl.multiple_of((v & 7) * TILE, TILE), TILE), :].astype(f32)
+            feat4 = jnp.concatenate([feat] * 4, axis=0).T
+            wide = jnp.concatenate([feat4] * (chunk // F), axis=1)
+            for s in range(0, PAIRS, chunk):
+                streams.append(dict(e=e, v=v, adj=adj, wide=wide, lanes=pl.ds(s, chunk)))
+        for x in streams:
+            x['off'] = dist_ref[pl.ds(x['e'], 1), x['lanes']] - centres
+            x['basis'] = jnp.exp(-sharp * x['off'] * x['off'])
+            x['inputs'] = jnp.concatenate([x['basis'].astype(bf16), ones], axis=0)
+            x['half'] = dot(w1, x['inputs'])
+            hi, lo = split(env_ref[pl.ds(x['e'], 1), x['lanes']])
+            member = rep_ref[:, x['lanes']]
+            spread = jnp.concatenate([member * hi, member * lo], axis=0)
+            x['adj_env'] = dot(x['adj'], spread, TN)
+        for x in streams:
+            x['t'] = jnp.tanh(x['half'])
+            x['soft_b'] = jnp.concatenate([jnp.log(1.0 - x['t']).astype(bf16), ones], axis=0)
+            x['d_raw_b'] = (x['adj_env'] * x['wide']).astype(bf16)
+        for x in streams:
+            x['filt'] = dot(nwft, x['soft_b'])
+            x['d_soft'] = dot(hwf, x['d_raw_b'])
+        for x in streams:
+            x['d_pre_b'] = (x['d_soft'] * (1.0 + x['t'])).astype(bf16)
+            x['y'] = x['adj_env'] * x['filt']
+            x['z_b'] = (x['y'] * x['wide']).astype(bf16)
         gw1 = jnp.zeros((F + NRBF, F), f32)
         gw2 = jnp.zeros((2 * NRBF, F), f32)
-        for s in range(0, PAIRS, chunk):
-            lanes = pl.ds(s, chunk)
-            dist_r = dist_ref[pl.ds(e, 1), lanes]
-            env_r = env_ref[pl.ds(e, 1), lanes]
-            off = dist_r - centres
-            basis = jnp.exp(-sharp * off * off)
-            inputs = jnp.concatenate([basis.astype(bf16), ones], axis=0)
-            half = dot(w1, inputs)
-            t = jnp.tanh(half)
-            soft_b = jnp.concatenate([jnp.log(1.0 - t).astype(bf16), ones], axis=0)
-            env_hi, env_lo = split(env_r)
-            member = rep_ref[:, lanes]
-            spread = jnp.concatenate([member * env_hi, member * env_lo], axis=0)
-            adj_env = dot(adj, spread, TN)
-            d_raw_b = (adj_env * wide).astype(bf16)
-            filt = dot(nwft, soft_b)
-            d_soft = dot(hwf, d_raw_b)
-            d_pre_b = (d_soft * (1.0 + t)).astype(bf16)
-            y = adj_env * filt
-            for q in range(0, chunk, F):
-                acc = acc + y[:, q:q + F]
-            z_b = (y * wide).astype(bf16)
-            zsum = dot(one_row, z_b)[0:1]
-            d_basis = dot(wr, d_pre_b)
-            d_dist = jnp.sum(d_basis * basis * off, axis=0, keepdims=True) * (-2.0 * sharp)
-            dd_ref[pl.ds(e, 1), lanes] = d_dist + tan_ref[pl.ds(e, 1), lanes] * zsum
-            gw1 = gw1 + dot(soft_b, d_raw_b, NT)
-            gw2 = gw2 + dot(inputs, d_pre_b, NT)
-        gf_ref[v] += dot(fold, jnp.concatenate(split(acc), axis=1), NT)
+        for x in streams:
+            zsum = dot(one_row, x['z_b'])[0:1]
+            d_basis = dot(wr, x['d_pre_b'])
+            d_dist = jnp.sum(d_basis * x['basis'] * x['off'], axis=0, keepdims=True) * (-2.0 * sharp)
+            x['dd'] = d_dist + tan_ref[pl.ds(x['e'], 1), x['lanes']] * zsum
+            gw1 = gw1 + dot(x['soft_b'], x['d_raw_b'], NT)
+            gw2 = gw2 + dot(x['inputs'], x['d_pre_b'], NT)
+        for e in entries:
+            acc = jnp.zeros((F, F), f32)
+            for x in streams:
+                if x['e'] is e:
+                    v = x['v']
+                    dd_ref[pl.ds(e, 1), x['lanes']] = x['dd']
+                    for q in range(0, chunk, F):
+                        acc = acc + x['y'][:, q:q + F]
+            gf_ref[v] += dot(fold, jnp.concatenate(split(acc), axis=1), NT)
         gw_ref[0:9] += gw1.reshape(9, WROWS, F)
         gw_ref[9:11] += gw2.reshape(2, WROWS, F)
         return carry
 
-    lax.fori_loop(0, count, body, 0)
+    lax.fori_loop(0, (count + tiles - 1) // tiles, body, 0)
 
     radial = dd_ref[...] / dist_ref[...]
-    rrow = row_ref[0:1]
-    srow = row_ref[1:2]
     t_sums = [jnp.zeros((48, F), f32), jnp.zeros((48, F), f32)]
     p_sums = [jnp.zeros((256, F), f32), jnp.zeros((256, F), f32)]
     for d in range(3):
         hi, lo = split(disp_ref[d] * radial)
         recv = dot(hi, rep4, NT) + dot(lo, rep4, NT)
         send = -(dot(hi, til4, NT) + dot(lo, til4, NT))
-        put_u = (rrow // 8 * 16 + d == iota((48, ROWS), 0)).astype(bf16)
-        put_v = (srow // 8 * 16 + d == iota((256, ROWS), 0)).astype(bf16)
+        put_u = ((rrow >> 3) * 16 + d == iota((48, ROWS), 0)).astype(bf16)
+        put_v = ((srow >> 3) * 16 + d == iota((256, ROWS), 0)).astype(bf16)
         for k, mask in enumerate((in_low_u, in_up_u)):
             hi, lo = split(jnp.where(mask, recv, 0.0))
             t_sums[k] = t_sums[k] + dot(put_u, hi) + dot(put_u, lo)
@@ -166,29 +199,17 @@
     gw_ref[11] = jnp.full((WROWS, F), count, jnp.int32).astype(f32)
 
 
-def parts_of(x):
-    hi = x.astype(bf16)
-    rest = x - hi.astype(f32)
-    mid = rest.astype(bf16)
-    low = (rest - mid.astype(f32)).astype(bf16)
-    return [hi, mid, low]
-
-
-def pairs(count, tower_tiles, plate_tiles, shifts, tower, plate, w_rbf, b_rbf, w_filter, b_filter, chunk=256):
-    padded = jnp.pad(jnp.stack([tower_tiles, plate_tiles, shifts]), ((0, 0), (0, ROWS - MAXT)))
-    zeros = [jnp.zeros((F,), bf16)] * (NRBF - 3)
-    w1 = jnp.concatenate([(w_rbf * 0.5).T, jnp.stack(parts_of(b_rbf * 0.5) + zeros, axis=1)], axis=1)
-    nwft = jnp.concatenate([-w_filter.T, jnp.stack(parts_of(b_filter) + zeros, axis=1)], axis=1)
+def pairs(count, tower_tiles, plate_tiles, shifts, tower, plate, w_rbf, b_rbf, w_filter, b_filter, chunk=256, tiles=2):
     smem = pl.BlockSpec(memory_space=pltpu.SMEM)
     vmem = pl.BlockSpec(memory_space=pltpu.VMEM)
     return pl.pallas_call(
-        lambda *refs: pairs_kernel(*refs, chunk=chunk),
+        lambda *refs: pairs_kernel(*refs, chunk=chunk, tiles=tiles),
         out_shape=(
             jax.ShapeDtypeStruct((BRICKS, PACK, F), bf16),
             jax.ShapeDtypeStruct((3, 32, F), f32),
             jax.ShapeDtypeStruct((16, WROWS, F), f32),
         ),
-        in_specs=[smem] * 3 + [vmem] * 8,
+        in_specs=[smem] * 3 + [vmem] * 9,
         out_specs=[vmem] * 3,
         scratch_shapes=[
             pltpu.VMEM((3, ROWS, PAIRS), f32),
@@ -198,10 +219,11 @@
             pltpu.VMEM((ROWS, PAIRS), f32),
             pltpu.VMEM((TILE, PAIRS), bf16),
             pltpu.VMEM((PLATE, TILE, F), f32),
+            pltpu.VMEM((8, F), f32),
         ],
-        compiler_params=pltpu.CompilerParams(vmem_limit_bytes=40 << 20),
+        compiler_params=pltpu.CompilerParams(vmem_limit_bytes=48 << 20),
         name="pairs",
-    )(count, tower_tiles, plate_tiles, tower, plate, padded.T, padded, w1, w_rbf, nwft, w_filter * jnp.asarray(0.5, bf16))
+    )(count, tower_tiles, plate_tiles, tower, plate, tower_tiles, plate_tiles, shifts, w_rbf, b_rbf.reshape(1, F), w_filter, b_filter.reshape(1, F))
 
 
 def send_to(src, dst, sends, recvs, slot, device):
@@ -347,7 +369,7 @@
 def local(features, adjoint, positions, w_rbf, b_rbf, w_filter, b_filter, atom_counts, tile_counts, tower_tiles, plate_tiles, image_shifts):
     plate, tower = gather(atom_counts[0], features[0], adjoint[0], positions[:, 0, :])
     pack, tg, gw = pairs(
-        tile_counts[0], tower_tiles[0, 0], plate_tiles[0, 0], image_shifts[0, 0],
+        tile_counts, tower_tiles, plate_tiles, image_shifts,
         tower, plate, w_rbf, b_rbf, w_filter, b_filter,
     )
     gf, gp, wr, br, wf, bf = reduce(atom_counts[0], pack, tg, gw)

time: 152 us -> 95.8 us (0.63)
  Pallas kernels: 140 us -> 83 us
  local copies, waits for them, and re-layouts: 5.72 us -> 10.6 us
  other arithmetic: 3.56 us -> 0 us
    pallas_call x1, Pallas kernels: 50.3 us -> 21.6 us  [pairs(): pl.pallas_call(lambda *refs: pairs_kernel(*refs, chunk=chunk, tiles=tiles...]
    pallas_call x1, Pallas kernels: 68.4 us -> 40 us  [reduce(): pl.pallas_call(reduce_kernel, out_shape=(jax.ShapeDtypeStruct((ATOMS, F),...]
    unnamed x19 -> x26, local copies, waits for them, and re-layouts: 4.38 us -> 10.6 us
    another operation x3 -> x0, other arithmetic: 2.09 us -> none  [the longest x1 0.73 us: pairs(): jnp.stack(parts_of(b_filter) + zeros, axis=1)]
where the time goes in v3:
time: 95.8 us; the launch traced here: 95.5 us
  Pallas kernels  83 us (87%)
  local copies, waits for them, and re-layouts  10.6 us (11%)
  between operations  1.98 us (2%)
    pallas_call x1, Pallas kernels, reduce(): pl.pallas_call(reduce_kernel, out_shape=(jax.ShapeDtypeStruct((ATOMS, F),...  40 us
    pallas_call x1, Pallas kernels, pairs(): pl.pallas_call(lambda *refs: pairs_kernel(*refs, chunk=chunk, tiles=tiles...  21.6 us
    pallas_call x1, Pallas kernels, gather(): pl.pallas_call(gather_kernel, out_shape=(jax.ShapeDtypeStruct((BRICKS, PA...  21.4 us
    unnamed x26, local copies, waits for them, and re-layouts  10.6 us

profile of v3, /device:TPU:1, one launch (start us, length us, event | category | flops | bytes accessed | tf_op | source)
XLA Modules:
  0.0 95.5 jit_solution(13941493130692591969)
XLA Ops:
  1.9 0.0 copy-start
  1.9 0.8 copy-done
  2.8 0.0 copy-start.1
  2.8 0.8 copy-done.1
  3.6 0.0 copy-start.4
  3.6 0.7 copy-done.4
  4.3 21.4 %gather.1 = (bf16[16,288,128]{2,1,0:T(8,128)(2,1)S(1)}, bf16[3,288,128]{2,1,0:T(8,128)(2,1)S(1)}) custom-call(s32[1]{0:T(128)} %bitcast.10.cnt_s, bf16[256,128]{1,0:T(8,128)(2,1)S(1)} %bitcast.13, bf16[256,128]{1,0:T(8,128)(2,1)S(1)} %bitcast.14, bf16[3,256]{1,0:T(4,128)(2,1)S(1)} %bitcast.16), custom_call_target="tpu_custom_call" | custom-call | tf_op jit(solution)/shard_map/gather/pallas_call | solution.py:281
  25.7 0.0 copy-start.2
  25.7 0.7 copy-done.2
  26.4 0.0 copy-start.3
  26.4 0.7 copy-done.3
  27.1 0.0 copy-start.5
  27.1 0.7 copy-done.5
  27.8 0.0 copy-start.6
  27.8 0.7 copy-done.6
  28.4 0.0 copy-start.7
  28.4 0.7 copy-done.7
  29.1 0.0 copy-start.8
  29.1 0.7 copy-done.8
  29.7 0.0 copy-start.9
  29.7 0.7 copy-done.9
  30.4 21.6 %pairs.1 = (bf16[16,288,128]{2,1,0:T(8,128)(2,1)S(1)}, f32[3,32,128]{2,1,0:T(8,128)S(1)}, f32[16,16,128]{2,1,0:T(8,128)S(1)}) custom-call(s32[1,1]{1,0:T(1,128)S(6)} %copy.25.refs_0_, s32[1,1,56]{2,1,0:T(1,128)S(1)} %copy-done.5, s32[1,1,56]{2,1,0:T(1,128)S(1)} %copy-done.6, bf16[3,288,128]{2,1,0:T(8,128)(2,1)S(1)} %get-tuple-element.17.refs_3_, ...), custom_call_target="tpu_custom_call" | custom-call | tf_op jit(solution)/shard_map/pairs/pallas_call | solution.py:205
  52.0 40.0 %reduce.1 = (f32[256,128]{1,0:T(8,128)S(1)}, f32[3,256]{1,0:T(4,128)S(1)}, f32[16,128]{1,0:T(8,128)S(1)}, f32[1,128]{1,0:T(1,128)S(1)}, f32[128,128]{1,0:T(8,128)S(1)}, /*index=5*/f32[1,128]{1,0:T(1,128)S(1)}) custom-call(s32[1]{0:T(128)} %bitcast.11.cnt_s, bf16[16,288,128]{2,1,0:T(8,128)(2,1)S(1)} %get-tuple-element.19.pack_ref, ...), custom_call_target="tpu_custom_call" | custom-call | tf_op jit(solution)/shard_map/reduce/pallas_call | solution.py:352
  92.0 0.6 copy.18
  92.6 0.7 copy.26
  93.2 0.6 copy.27
  93.8 0.5 copy.28
  94.3 0.6 copy.29
  95.0 0.5 copy.30
Async XLA Ops:
  1.9 0.8 copy-start
  2.8 0.8 copy-start.1
  3.6 0.7 copy-start.4
  25.7 0.8 copy-start.2
  26.4 0.7 copy-start.3
  27.1 0.7 copy-start.5
  27.8 0.7 copy-start.6
  28.4 0.7 copy-start.7
  29.1 0.7 copy-start.8
  29.7 0.7 copy-start.9

commit v4 on v3

v4 whole, which is shorter than its diff:
```python
import math

import jax
import jax.numpy as jnp
from jax import lax
from jax.experimental import pallas as pl
from jax.experimental.pallas import tpu as pltpu

F = 128
TILE = 32
PAIRS = TILE * TILE
MAXT = 56
ATOMS = 256
PACK = ATOMS + 16
BRICKS = 16
WROWS = 16
ROWS = 64
TOWER = 24
PLATE = 128
NRBF = 16
cutoff = 3.0
soften = 0.01
sharp = 10.0
f32 = jnp.float32
bf16 = jnp.bfloat16

NN = (((1,), (0,)), ((), ()))
NT = (((1,), (1,)), ((), ()))
TN = (((0,), (0,)), ((), ()))


def dot(a, b, dims=NN):
    return lax.dot_general(a, b, dims, preferred_element_type=f32)


def iota(shape, axis):
    return lax.broadcasted_iota(jnp.int32, shape, axis)


def split(x):
    hi = x.astype(bf16)
    return hi, (x - hi.astype(f32)).astype(bf16)


def sine(x):
    y = x * x
    acc = jnp.full_like(x, 1.0 / 6227020800.0)
    for c in (-1.0 / 39916800.0, 1.0 / 362880.0, -1.0 / 5040.0, 1.0 / 120.0, -1.0 / 6.0, 1.0):
        acc = acc * y + c
    return acc * x


def three(x):
    hi = x.astype(bf16).astype(f32)
    mid = (x - hi).astype(bf16).astype(f32)
    return [hi, mid, x - hi - mid]


def pairs_kernel(
    cnt_s,
    tower_ref, plate_ref, u_ref, v_ref, c_ref,
    wr_ref, br_ref, wf_ref, bf_ref,
    pack_ref, tg_ref, gw_ref,
    disp_ref, dist_ref, env_ref, tan_ref, dd_ref, rep_ref, gf_ref, list_ref, sum_ref, u_s, v_s, list_sem,
    *, chunk, tiles,
):
    count = cnt_s[0, 0]
    lists_in = [pltpu.make_async_copy(u_ref, u_s, list_sem.at[0]), pltpu.make_async_copy(v_ref, v_s, list_sem.at[1])]
    for copy in lists_in:
        copy.start()
    list_ref[...] = jnp.zeros(list_ref.shape, f32)
    for k, ref in enumerate((u_ref, v_ref, c_ref)):
        list_ref[k:k + 1, 0:MAXT] = ref[0].astype(f32)
    lists = list_ref[...]
    columns = lists.T.astype(jnp.int32)
    rrow = lists[0:1, 0:ROWS].astype(jnp.int32)
    srow = lists[1:2, 0:ROWS].astype(jnp.int32)
    ucol = columns[0:ROWS, 0:1]
    vcol = columns[0:ROWS, 1:2]
    ccol = columns[0:ROWS, 2:3]
    rep = (iota((TILE, PAIRS), 1) >> 5 == iota((TILE, PAIRS), 0)).astype(bf16)
    rep_ref[...] = rep
    rep4 = (iota((F, PAIRS), 1) >> 5 == (iota((F, PAIRS), 0) & 31)).astype(bf16)
    til4 = ((iota((F, PAIRS), 1) & 31) == (iota((F, PAIRS), 0) & 31)).astype(bf16)
    group = iota((ROWS, F), 1) >> 5
    in_u = group == (ucol & 3)
    in_v = group == (vcol & 3)
    row_u = (ucol >> 3) * 16 + ((ucol >> 2) & 1) * 3
    row_v = (vcol >> 3) * 16 + ((vcol >> 2) & 1) * 3
    t_pos = tower_ref[:, ATOMS:PACK, :].reshape(48, F)
    p_pos = plate_ref[:, ATOMS:PACK, :].reshape(256, F)
    third = (ccol >= 3).astype(jnp.int32) + (ccol >= 6).astype(jnp.int32)
    shifts = (third - 1, ccol - 3 * third - 1, (ucol >> 3) - 1)
    square = jnp.zeros((ROWS, PAIRS), f32)
    for d in range(3):
        pick_u = (row_u + d == iota((ROWS, 48), 1)).astype(bf16)
        pick_v = (row_v + d == iota((ROWS, 256), 1)).astype(bf16)
        recv = jnp.where(in_u, dot(pick_u, t_pos), 0.0)
        send = jnp.where(in_v, dot(pick_v, p_pos), 0.0)
        disp = dot(recv.astype(bf16), rep4) - dot(send.astype(bf16), til4) + shifts[d].astype(f32)
        disp_ref[d] = disp
        square = square + disp * disp
    dist = jnp.sqrt(square + soften)
    dist_ref[...] = dist
    inside = (dist < cutoff) & (iota((ROWS, PAIRS), 0) < count)
    theta = jnp.minimum(dist, cutoff) * (math.pi / (2 * cutoff))
    cosine = jnp.maximum(sine(math.pi / 2 - theta), 1e-6)
    env_ref[...] = jnp.where(inside, cosine * cosine, 0.0)
    tan_ref[...] = jnp.where(inside, (-math.pi / cutoff) * sine(theta) / cosine, 0.0)
    dd_ref[...] = jnp.zeros((ROWS, PAIRS), f32)
    gf_ref[...] = jnp.zeros(gf_ref.shape, f32)
    sum_ref[...] = jnp.zeros(sum_ref.shape, f32)

    centres = iota((NRBF, 1), 0).astype(f32) * (cutoff / (NRBF - 1))
    ones = jnp.ones((NRBF, chunk), bf16)
    wr = wr_ref[...]
    zeros = jnp.zeros((NRBF - 3, F), f32)
    w1 = jnp.concatenate([wr.astype(f32) * 0.5] + three(br_ref[...] * 0.5) + [zeros], axis=0).T.astype(bf16)
    wf = wf_ref[...].astype(f32)
    nwft = jnp.concatenate([-wf.T, jnp.concatenate(three(bf_ref[...]) + [zeros], axis=0).T], axis=1).astype(bf16)
    hwf = (wf * 0.5).astype(bf16)
    fold = ((iota((TILE, 2 * F), 1) & 31) == iota((TILE, 2 * F), 0)).astype(bf16)

    def body(step, carry):
        entries = [step * tiles + k for k in range(tiles)]
        streams = []
        for e in entries:
            listed = jnp.minimum(e, MAXT - 1)
            u = u_s[0, 0, listed]
            v = v_s[0, 0, listed]
            adj = tower_ref[u >> 3, pl.ds(pl.multiple_of((u & 7) * TILE, TILE), TILE), :]
            adj = jnp.concatenate([adj] * 2, axis=0)
            feat = plate_ref[v >> 3, pl.ds(pl.multiple_of((v & 7) * TILE, TILE), TILE), :].astype(f32)
            feat4 = jnp.concatenate([feat] * 4, axis=0).T
            wide = jnp.concatenate([feat4] * (chunk // F), axis=1)
            for s in range(0, PAIRS, chunk):
                streams.append(dict(e=e, v=v, adj=adj, wide=wide, lanes=pl.ds(s, chunk)))
        for x in streams:
            x['off'] = dist_ref[pl.ds(x['e'], 1), x['lanes']] - centres
            x['basis'] = jnp.exp(-sharp * x['off'] * x['off'])
            x['inputs'] = jnp.concatenate([x['basis'].astype(bf16), ones], axis=0)
            x['half'] = dot(w1, x['inputs'])
            hi, lo = split(env_ref[pl.ds(x['e'], 1), x['lanes']])
            member = rep_ref[:, x['lanes']]
            spread = jnp.concatenate([member * hi, member * lo], axis=0)
            x['adj_env'] = dot(x['adj'], spread, TN)
        for x in streams:
            x['t'] = jnp.tanh(x['half'])
            x['soft_b'] = jnp.concatenate([jnp.log(1.0 - x['t']).astype(bf16), ones], axis=0)
            x['d_raw_b'] = (x['adj_env'] * x['wide']).astype(bf16)
        for x in streams:
            x['filt'] = dot(nwft, x['soft_b'])
            x['d_soft'] = dot(hwf, x['d_raw_b'])
        for x in streams:
            x['d_pre_b'] = (x['d_soft'] * (1.0 + x['t'])).astype(bf16)
            x['y'] = x['adj_env'] * x['filt']
            x['zsum'] = jnp.sum(x['y'] * x['wide'], axis=0, keepdims=True)
        gw = jnp.zeros((2 * F, F + 2 * NRBF), f32)
        for x in streams:
            d_basis = dot(wr, x['d_pre_b'])
            d_dist = jnp.sum(d_basis * x['basis'] * x['off'], axis=0, keepdims=True) * (-2.0 * sharp)
            x['dd'] = d_dist + tan_ref[pl.ds(x['e'], 1), x['lanes']] * x['zsum']
            grads = jnp.concatenate([x['d_raw_b'], x['d_pre_b']], axis=0)
            values = jnp.concatenate([x['soft_b'], x['inputs'][0:NRBF]], axis=0)
            gw = gw + dot(grads, values, NT)
        for e in entries:
            acc = jnp.zeros((F, F), f32)
            for x in streams:
                if x['e'] is e:
                    v = x['v']
                    dd_ref[pl.ds(e, 1), x['lanes']] = x['dd']
                    for q in range(0, chunk, F):
                        acc = acc + x['y'][:, q:q + F]
            gf_ref[v] += dot(fold, jnp.concatenate(split(acc), axis=1), NT)
        sum_ref[...] += gw
        return carry

    for copy in lists_in:
        copy.wait()
    lax.fori_loop(0, (count + tiles - 1) // tiles, body, 0)

    radial = dd_ref[...] / dist_ref[...]
    t_sum = jnp.zeros((48, F), f32)
    p_sum = jnp.zeros((256, F), f32)
    to_u = (rrow >> 3) * 16 + ((rrow >> 2) & 1) * 3
    to_v = (srow >> 3) * 16 + ((srow >> 2) & 1) * 3
    for d in range(3):
        hi, lo = split(disp_ref[d] * radial)
        recv_hi, recv_lo = split(jnp.where(in_u, dot(hi, rep4, NT) + dot(lo, rep4, NT), 0.0))
        send_hi, send_lo = split(jnp.where(in_v, dot(hi, til4, NT) + dot(lo, til4, NT), 0.0))
        put_u = (to_u + d == iota((48, ROWS), 0)).astype(bf16)
        put_v = (to_v + d == iota((256, ROWS), 0)).astype(bf16)
        t_sum = t_sum + dot(put_u, recv_hi) + dot(put_u, recv_lo)
        p_sum = p_sum - dot(put_v, send_hi) - dot(put_v, send_lo)
    tg_ref[...] = t_sum.reshape(3, 16, F)
    pack_ref[:, ATOMS:PACK, :] = p_sum.astype(bf16).reshape(BRICKS, 16, F)
    pack_ref[:, 0:ATOMS, :] = gf_ref[...].reshape(BRICKS, ATOMS, F).astype(bf16)
    gw_ref[0:8] = sum_ref[0:F, 0:F].T.reshape(8, WROWS, F)
    gw_ref[8] = sum_ref[0:F, F:F + 2 * NRBF].T[0:WROWS]
    rest = sum_ref[F:2 * F, F:F + 2 * NRBF].T
    gw_ref[9] = rest[NRBF:2 * NRBF]
    gw_ref[10] = rest[0:NRBF]
    gw_ref[12:16] = jnp.zeros((4, WROWS, F), f32)
    gw_ref[11] = jnp.full((WROWS, F), count, jnp.int32).astype(f32)


def pairs(count, tower, plate, params, chunk=256, tiles=2):
    smem = pl.BlockSpec(memory_space=pltpu.SMEM)
    vmem = pl.BlockSpec(memory_space=pltpu.VMEM)
    return pl.pallas_call(
        lambda *refs: pairs_kernel(*refs, chunk=chunk, tiles=tiles),
        out_shape=(
            jax.ShapeDtypeStruct((BRICKS, PACK, F), bf16),
            jax.ShapeDtypeStruct((3, 16, F), f32),
            jax.ShapeDtypeStruct((16, WROWS, F), f32),
        ),
        in_specs=[smem] + [vmem] * 9,
        out_specs=[vmem] * 3,
        scratch_shapes=[
            pltpu.VMEM((3, ROWS, PAIRS), f32),
            pltpu.VMEM((ROWS, PAIRS), f32),
            pltpu.VMEM((ROWS, PAIRS), f32),
            pltpu.VMEM((ROWS, PAIRS), f32),
            pltpu.VMEM((ROWS, PAIRS), f32),
            pltpu.VMEM((TILE, PAIRS), bf16),
            pltpu.VMEM((PLATE, TILE, F), f32),
            pltpu.VMEM((8, F), f32),
            pltpu.VMEM((2 * F, F + 2 * NRBF), f32),
            pltpu.SMEM((1, 1, MAXT), jnp.int32),
            pltpu.SMEM((1, 1, MAXT), jnp.int32),
            pltpu.SemaphoreType.DMA((2,)),
        ],
        compiler_params=pltpu.CompilerParams(vmem_limit_bytes=48 << 20),
        name="pairs",
    )(count, tower, plate, *params)


def send_to(src, dst, sends, recvs, slot, device):
    copy = pltpu.make_async_remote_copy(
        src_ref=src, dst_ref=dst, send_sem=sends.at[slot], recv_sem=recvs.at[slot],
        device_id=device, device_id_type=pl.DeviceIdType.MESH,
    )
    copy.start()
    return copy


def greet(devices):
    barrier = pltpu.get_barrier_semaphore()
    for device in devices:
        pl.semaphore_signal(barrier, inc=1, device_id=device, device_id_type=pl.DeviceIdType.MESH)
    pl.semaphore_wait(barrier, len(devices))


def gather_kernel(
    cnt_s, feat_hbm, adj_hbm, pos_hbm, *refs,
):
    params_hbm, (plate_ref, tower_ref), params = refs[:7], refs[7:9], refs[9:16]
    feat_ref, adj_ref, pos_ref, local_sem, chip_send, chip_recv, mate_send, mate_recv, tower_send, tower_recv = refs[16:]
    t = lax.axis_index("tower")
    p = lax.axis_index("plate")
    q, core = p // 2, p % 2
    mate = (t, q * 2 + 1 - core)
    above = ((t + 1) % 16, p)
    below = ((t + 15) % 16, p)
    chips = [(q + d) % 8 for d in range(8)]
    back = [(q + 8 - d) % 8 for d in range(8)]
    local = []
    for k, (src, dst) in enumerate(zip((feat_hbm, adj_hbm, pos_hbm) + params_hbm, (feat_ref, adj_ref, pos_ref) + params)):
        local.append(pltpu.make_async_copy(src, dst, local_sem.at[k]))
        local[k].start()
    barrier = pltpu.get_barrier_semaphore()
    peers = [(t, chips[d] * 2 + core) for d in range(1, 8)] + [mate, above, below]
    for device in peers:
        pl.semaphore_signal(barrier, inc=1, device_id=device, device_id_type=pl.DeviceIdType.MESH)
    local[0].wait()
    local[1].wait()
    local[2].wait()
    live = iota((ATOMS, F), 0) < cnt_s[0, 0]
    halves = [pos_ref[:, k * F:(k + 1) * F].astype(f32) for k in range(2)]
    rows = jnp.concatenate(halves + [jnp.zeros((10, F), f32)], axis=0).astype(bf16)
    for src, ref, slot in ((feat_ref, plate_ref, p), (adj_ref, tower_ref, 1)):
        ref[slot, 0:ATOMS, :] = jnp.where(live, src[...].astype(f32), 0.0).astype(bf16)
        ref[slot, ATOMS:PACK, :] = rows
    pl.semaphore_wait(barrier, len(peers))
    mine = plate_ref.at[p]
    out = [send_to(mine, mine, chip_send, chip_recv, d, (t, chips[d] * 2 + core)) for d in range(1, 8)]
    out.append(send_to(mine, mine, mate_send, mate_recv, 0, mate))
    up = send_to(tower_ref.at[1], tower_ref.at[0], tower_send, tower_recv, 0, above)
    down = send_to(tower_ref.at[1], tower_ref.at[2], tower_send, tower_recv, 1, below)
    passed = []
    for d in range(1, 8):
        out[d - 1].wait_recv()
        block = plate_ref.at[back[d] * 2 + core]
        passed.append(send_to(block, block, mate_send, mate_recv, d, mate))
    for copy in local[3:]:
        copy.wait()
    for copy in out:
        copy.wait_send()
    out[7].wait_recv()
    for copy in passed + [up, down]:
        copy.wait()


def gather(count, feat, adj, pos, params):
    smem = pl.BlockSpec(memory_space=pltpu.SMEM)
    vmem = pl.BlockSpec(memory_space=pltpu.VMEM)
    hbm = pl.BlockSpec(memory_space=pltpu.HBM)
    out = pl.pallas_call(
        gather_kernel,
        out_shape=[jax.ShapeDtypeStruct((BRICKS, PACK, F), bf16), jax.ShapeDtypeStruct((3, PACK, F), bf16)]
        + [jax.ShapeDtypeStruct(x.shape, x.dtype) for x in params],
        in_specs=[smem] + [hbm] * 10,
        out_specs=[vmem] * 9,
        scratch_shapes=[pltpu.VMEM((ATOMS, F), bf16), pltpu.VMEM((ATOMS, F), bf16), pltpu.VMEM((3, ATOMS), bf16), pltpu.SemaphoreType.DMA((10,))]
        + [pltpu.SemaphoreType.DMA((8,))] * 4 + [pltpu.SemaphoreType.DMA((2,))] * 2,
        compiler_params=pltpu.CompilerParams(collective_id=0, has_side_effects=True, vmem_limit_bytes=24 << 20),
        name="gather",
    )(count, feat, adj, pos, *params)
    return out[0], out[1], out[2:]


def reduce_kernel(
    pack_ref, tg_ref, gw_ref, acc_ref, w3_buf,
    mate_buf, send_buf, chip_buf, tower_buf, w1_buf, w2_own, w2_buf,
    mate_send, mate_recv, chip_send, chip_recv, tower_send, tower_recv, w_send, w_recv,
):
    t = lax.axis_index("tower")
    p = lax.axis_index("plate")
    q, core = p // 2, p % 2
    mate = (t, q * 2 + 1 - core)
    chips = [(q + d) % 8 for d in range(8)]
    plate = [(t, (p + d) % 16) for d in range(16)]
    tower = [((t + d) % 16, p) for d in range(16)]
    greet(plate[1:] + tower[1:])
    first = [send_to(gw_ref.at[(p + d) % 16], w1_buf.at[d], w_send.at[0], w_recv.at[0], d, plate[d]) for d in range(1, 16)]
    halves = [send_to(pack_ref.at[chips[d] * 2 + 1 - core], mate_buf.at[d], mate_send, mate_recv, d, mate) for d in (1, 2, 3, 4, 5, 6, 7, 0)]
    up = send_to(tg_ref.at[2], tower_buf.at[0], tower_send, tower_recv, 0, tower[1])
    down = send_to(tg_ref.at[0], tower_buf.at[1], tower_send, tower_recv, 1, tower[15])
    total = gw_ref[p]
    for d in range(1, 16):
        first[d - 1].wait_recv()
        total = total + w1_buf[d]
    w2_own[...] = total
    second = [send_to(w2_own, w2_buf.at[d], w_send.at[1], w_recv.at[1], d, tower[d]) for d in range(1, 16)]
    chip = []
    for d in range(1, 8):
        halves[d - 1].wait_recv()
        send_buf[d] = (pack_ref[chips[d] * 2 + core].astype(f32) + mate_buf[d].astype(f32)).astype(bf16)
        chip.append(send_to(send_buf.at[d], chip_buf.at[d], chip_send, chip_recv, d, (t, chips[d] * 2 + core)))
    for d in range(1, 16):
        second[d - 1].wait_recv()
        total = total + w2_buf[d]
    w3_buf[p] = total
    third = [send_to(w3_buf.at[p], w3_buf.at[p], w_send.at[2], w_recv.at[2], d, plate[d]) for d in range(1, 16)]
    halves[7].wait_recv()
    acc = pack_ref[p].astype(f32) + mate_buf[0].astype(f32)
    for d in range(1, 8):
        chip[d - 1].wait_recv()
        acc = acc + chip_buf[d].astype(f32)
    acc_ref[0:ATOMS, :] = acc[0:ATOMS]
    up.wait_recv()
    down.wait_recv()
    acc_ref[ATOMS:PACK, :] = acc[ATOMS:PACK] + tg_ref[1] + tower_buf[0] + tower_buf[1]
    for d in range(1, 16):
        third[d - 1].wait_recv()
    for copy in first + halves + [up, down] + second + chip + third:
        copy.wait_send()


def reduce(pack, tg, gw):
    vmem = pl.BlockSpec(memory_space=pltpu.VMEM)
    weights = pltpu.VMEM((16, WROWS, F), f32)
    dma = pltpu.SemaphoreType.DMA
    return pl.pallas_call(
        reduce_kernel,
        out_shape=(jax.ShapeDtypeStruct((PACK, F), f32), jax.ShapeDtypeStruct((16, WROWS, F), f32)),
        in_specs=[vmem] * 3,
        out_specs=[vmem] * 2,
        scratch_shapes=[pltpu.VMEM((8, PACK, F), bf16)] * 3 + [
            pltpu.VMEM((2, 16, F), f32), weights, pltpu.VMEM((WROWS, F), f32), weights,
            dma((8,)), dma((8,)), dma((8,)), dma((8,)), dma((2,)), dma((2,)), dma((3, 16)), dma((3, 16)),
        ],
        compiler_params=pltpu.CompilerParams(collective_id=1, has_side_effects=True, vmem_limit_bytes=24 << 20),
        name="reduce",
    )(pack, tg, gw)


def finish_kernel(cnt_s, acc_ref, w_ref, gf_out, gp_out, wr_out, br_out, wf_out, bf_out):
    gf_out[0] = jnp.where(iota((ATOMS, F), 0) < cnt_s[0, 0], acc_ref[0:ATOMS, :], 0.0)
    for k in range(2):
        for d in range(3):
            gp_out[d, :, k * F:(k + 1) * F] = acc_ref[ATOMS + 3 * k + d:ATOMS + 3 * k + d + 1, :]
    scale = lax.rsqrt(w_ref[11][0:1] * (TILE * TILE))
    wf_out[...] = w_ref[0:8].reshape(F, F) * -scale
    bf_out[...] = w_ref[8][0:1] * scale
    wr_out[...] = w_ref[9] * scale
    br_out[...] = w_ref[10][0:1] * scale


def finish(count, acc, weights):
    smem = pl.BlockSpec(memory_space=pltpu.SMEM)
    vmem = pl.BlockSpec(memory_space=pltpu.VMEM)
    return pl.pallas_call(
        finish_kernel,
        out_shape=(
            jax.ShapeDtypeStruct((1, ATOMS, F), f32), jax.ShapeDtypeStruct((3, 1, ATOMS), f32), jax.ShapeDtypeStruct((NRBF, F), f32),
            jax.ShapeDtypeStruct((1, F), f32), jax.ShapeDtypeStruct((F, F), f32), jax.ShapeDtypeStruct((1, F), f32),
        ),
        in_specs=[smem, vmem, vmem],
        out_specs=[vmem] * 6,
        compiler_params=pltpu.CompilerParams(vmem_limit_bytes=8 << 20),
        name="finish",
    )(count, acc, weights)


def local(features, adjoint, positions, w_rbf, b_rbf, w_filter, b_filter, atom_counts, tile_counts, tower_tiles, plate_tiles, image_shifts):
    params = [pltpu.with_memory_space_constraint(x, pltpu.HBM) for x in (tower_tiles, plate_tiles, image_shifts, w_rbf, b_rbf.reshape(1, F), w_filter, b_filter.reshape(1, F))]
    plate, tower, params = gather(atom_counts, *[pltpu.with_memory_space_constraint(x, pltpu.HBM) for x in (features[0], adjoint[0], positions[:, 0, :])], params)
    pack, tg, gw = pairs(tile_counts, tower, plate, params)
    gf, gp, wr, br, wf, bf = finish(atom_counts, *reduce(pack, tg, gw))
    return gf, gp, wr, br[0], wf, bf[0]


def solution(mesh):
    from jax.sharding import PartitionSpec as P
    brick = P("tower", "plate", None)
    one = P("tower", "plate")
    return jax.shard_map(
        local, mesh=mesh,
        in_specs=(brick, brick, P(None, "tower", "plate"), P(), P(), P(), P(), one, one, brick, brick, brick),
        out_specs=(brick, P(None, "tower", "plate"), P(), P(), P(), P()),
        check_vma=False,
    )
```

time: 95.8 us -> 80.9 us (0.84)
  local copies, waits for them, and re-layouts: 10.6 us -> 0 us
  Pallas kernels: 83 us -> 78.8 us
    unnamed x26 -> x0, local copies, waits for them, and re-layouts: 10.6 us -> none
    pallas_call x1, Pallas kernels: 21.6 us -> 11.2 us  [pairs(): pl.pallas_call(lambda *refs: pairs_kernel(*refs, chunk=chunk, tiles=tiles...]
    pallas_call x2 -> x3, Pallas kernels: 61.4 us -> 67.6 us  [the longest x1 45.8 us: reduce(): pl.pallas_call(reduce_kernel, out_shape=(jax.ShapeDtypeStruct((PACK, F),...]
where the time goes in v4:
time: 80.9 us; the launch traced here: 80.8 us
  Pallas kernels  78.8 us (97%)
  between operations  1.95 us (2%)
    pallas_call x1, Pallas kernels, reduce(): pl.pallas_call(reduce_kernel, out_shape=(jax.ShapeDtypeStruct((PACK, F),...  45.8 us
    pallas_call x1, Pallas kernels, gather(): pl.pallas_call(gather_kernel, out_shape=[jax.ShapeDtypeStruct((BRICKS, PA...  21.1 us
    pallas_call x1, Pallas kernels, pairs(): pl.pallas_call(lambda *refs: pairs_kernel(*refs, chunk=chunk, tiles=tiles...  11.2 us

profile of v4, /device:TPU:1, one launch (start us, length us, event | category | flops | bytes accessed | tf_op | source)
XLA Modules:
  0.0 80.8 jit_solution(1026232213192801624)
XLA Ops:
  1.9 21.1 %gather.1 = (bf16[16,272,128]{2,1,0:T(8,128)(2,1)S(1)}, bf16[3,272,128]{2,1,0:T(8,128)(2,1)S(1)}, s32[1,1,56]{2,1,0:T(1,128)S(1)}, s32[1,1,56]{2,1,0:T(1,128)S(1...) custom-call(s32[1,1]{1,0:T(1,128)S(6)} %copy.18.cnt_s, ...), custom_call_target="tpu_custom_call" | custom-call | tf_op jit(solution)/shard_map/gather/pallas_call | solution.py:308
  23.0 11.2 %pairs.1 = (bf16[16,272,128]{2,1,0:T(8,128)(2,1)S(1)}, f32[3,16,128]{2,1,0:T(8,128)S(1)}, f32[16,16,128]{2,1,0:T(8,128)S(1)}) custom-call(s32[1,1]{1,0:T(1,128)S(6)} %copy.19.refs_0_, bf16[3,272,128]{2,1,0:T(8,128)(2,1)S(1)} %get-tuple-element.26.refs_1_, bf16[16,272,128]{2,1,0:T(8,128)(2,1)S(1)} %get-tuple-element.27.refs_2_, ...), custom_call_target="tpu_custom_call" | custom-call | tf_op jit(solution)/shard_map/pairs/pallas_call | solution.py:210
  34.3 45.8 %reduce.1 = (f32[272,128]{1,0:T(8,128)S(1)}, f32[16,16,128]{2,1,0:T(8,128)S(1)}) custom-call(bf16[16,272,128]{2,1,0:T(8,128)(2,1)S(1)} %get-tuple-element.35.pack_ref, f32[3,16,128]{2,1,0:T(8,128)S(1)} %get-tuple-element.36.tg_ref, f32[16,16,128]{2,1,0:T(8,128)S(1)} %get-tuple-element.37.gw_ref), custom_call_target="tpu_custom_call" | custom-call | tf_op jit(solution)/shard_map/reduce/pallas_call | solution.py:374
  80.1 0.7 finish.1

commit v5 on v4

--- a/solution.py
+++ b/solution.py
@@ -61,7 +61,7 @@
     tower_ref, plate_ref, u_ref, v_ref, c_ref,
     wr_ref, br_ref, wf_ref, bf_ref,
     pack_ref, tg_ref, gw_ref,
-    disp_ref, dist_ref, env_ref, tan_ref, dd_ref, rep_ref, gf_ref, list_ref, sum_ref, u_s, v_s, list_sem,
+    disp_ref, dist_ref, env_ref, tan_ref, dd_ref, rep_ref, gf_ref, list_ref, sum_ref, u_s, v_s, flag_ref, flag_s, order_s, list_sem,
     *, chunk, tiles,
 ):
     count = cnt_s[0, 0]
@@ -91,6 +91,14 @@
     p_pos = plate_ref[:, ATOMS:PACK, :].reshape(256, F)
     third = (ccol >= 3).astype(jnp.int32) + (ccol >= 6).astype(jnp.int32)
     shifts = (third - 1, ccol - 3 * third - 1, (ucol >> 3) - 1)
+    pick_u = ((ucol >> 3) * 16 + 6 == iota((ROWS, 48), 1)).astype(bf16)
+    pick_v = ((vcol >> 3) * 16 + 6 == iota((ROWS, 256), 1)).astype(bf16)
+    first_u = ((ucol & 7) * TILE).astype(f32)
+    first_v = ((vcol & 7) * TILE).astype(f32)
+    live = (first_u < dot(pick_u, t_pos)) & (first_v < dot(pick_v, p_pos)) & (iota((ROWS, F), 0) < count)
+    flag_ref[...] = live.astype(f32).T[0:8].astype(jnp.int32)
+    flags = pltpu.make_async_copy(flag_ref, flag_s, list_sem.at[2])
+    flags.start()
     square = jnp.zeros((ROWS, PAIRS), f32)
     for d in range(3):
         pick_u = (row_u + d == iota((ROWS, 48), 1)).astype(bf16)
@@ -122,7 +130,7 @@
     fold = ((iota((TILE, 2 * F), 1) & 31) == iota((TILE, 2 * F), 0)).astype(bf16)
 
     def body(step, carry):
-        entries = [step * tiles + k for k in range(tiles)]
+        entries = [order_s[step * tiles + k] for k in range(tiles)]
         streams = []
         for e in entries:
             listed = jnp.minimum(e, MAXT - 1)
@@ -177,17 +185,29 @@
 
     for copy in lists_in:
         copy.wait()
-    lax.fori_loop(0, (count + tiles - 1) // tiles, body, 0)
+    flags.wait()
+
+    def keep(e, n):
+        order_s[n] = e
+        return n + flag_s[0, e]
+
+    kept = lax.fori_loop(0, MAXT, keep, 0)
+    for k in range(tiles - 1):
+        order_s[kept + k] = ROWS - 1
+    lax.fori_loop(0, (kept + tiles - 1) // tiles, body, 0)
 
     radial = dd_ref[...] / dist_ref[...]
     t_sum = jnp.zeros((48, F), f32)
     p_sum = jnp.zeros((256, F), f32)
     to_u = (rrow >> 3) * 16 + ((rrow >> 2) & 1) * 3
     to_v = (srow >> 3) * 16 + ((srow >> 2) & 1) * 3
+    pulls = jnp.concatenate([part for d in range(3) for part in split(disp_ref[d] * radial)], axis=0)
+    recv_all = dot(pulls, rep4, NT)
+    send_all = dot(pulls, til4, NT)
     for d in range(3):
-        hi, lo = split(disp_ref[d] * radial)
-        recv_hi, recv_lo = split(jnp.where(in_u, dot(hi, rep4, NT) + dot(lo, rep4, NT), 0.0))
-        send_hi, send_lo = split(jnp.where(in_v, dot(hi, til4, NT) + dot(lo, til4, NT), 0.0))
+        at = 2 * ROWS * d
+        recv_hi, recv_lo = split(jnp.where(in_u, recv_all[at:at + ROWS] + recv_all[at + ROWS:at + 2 * ROWS], 0.0))
+        send_hi, send_lo = split(jnp.where(in_v, send_all[at:at + ROWS] + send_all[at + ROWS:at + 2 * ROWS], 0.0))
         put_u = (to_u + d == iota((48, ROWS), 0)).astype(bf16)
         put_v = (to_v + d == iota((256, ROWS), 0)).astype(bf16)
         t_sum = t_sum + dot(put_u, recv_hi) + dot(put_u, recv_lo)
@@ -228,7 +248,10 @@
             pltpu.VMEM((2 * F, F + 2 * NRBF), f32),
             pltpu.SMEM((1, 1, MAXT), jnp.int32),
             pltpu.SMEM((1, 1, MAXT), jnp.int32),
-            pltpu.SemaphoreType.DMA((2,)),
+            pltpu.VMEM((8, ROWS), jnp.int32),
+            pltpu.SMEM((8, ROWS), jnp.int32),
+            pltpu.SMEM((ROWS,), jnp.int32),
+            pltpu.SemaphoreType.DMA((3,)),
         ],
         compiler_params=pltpu.CompilerParams(vmem_limit_bytes=48 << 20),
         name="pairs",
@@ -277,7 +300,8 @@
     local[2].wait()
     live = iota((ATOMS, F), 0) < cnt_s[0, 0]
     halves = [pos_ref[:, k * F:(k + 1) * F].astype(f32) for k in range(2)]
-    rows = jnp.concatenate(halves + [jnp.zeros((10, F), f32)], axis=0).astype(bf16)
+    atoms = jnp.full((1, F), cnt_s[0, 0], jnp.int32).astype(f32)
+    rows = jnp.concatenate(halves + [atoms, jnp.zeros((9, F), f32)], axis=0).astype(bf16)
     for src, ref, slot in ((feat_ref, plate_ref, p), (adj_ref, tower_ref, 1)):
         ref[slot, 0:ATOMS, :] = jnp.where(live, src[...].astype(f32), 0.0).astype(bf16)
         ref[slot, ATOMS:PACK, :] = rows

time: 80.9 us -> 76.9 us (0.951)
  Pallas kernels: 78.8 us -> 74.8 us
    pallas_call x1, Pallas kernels: 45.8 us -> 40.6 us  [reduce(): pl.pallas_call(reduce_kernel, out_shape=(jax.ShapeDtypeStruct((PACK, F),...]
    pallas_call x1, Pallas kernels: 11.2 us -> 12.4 us  [pairs(): pl.pallas_call(lambda *refs: pairs_kernel(*refs, chunk=chunk, tiles=tiles...]
where the time goes in v5:
time: 76.9 us; the launch traced here: 76.8 us
  Pallas kernels  74.8 us (97%)
  between operations  1.95 us (3%)
    pallas_call x1, Pallas kernels, reduce(): pl.pallas_call(reduce_kernel, out_shape=(jax.ShapeDtypeStruct((PACK, F),...  40.6 us
    pallas_call x1, Pallas kernels, gather(): pl.pallas_call(gather_kernel, out_shape=[jax.ShapeDtypeStruct((BRICKS, PA...  21.1 us
    pallas_call x1, Pallas kernels, pairs(): pl.pallas_call(lambda *refs: pairs_kernel(*refs, chunk=chunk, tiles=tiles...  12.4 us

profile of v5, /device:TPU:1, one launch (start us, length us, event | category | flops | bytes accessed | tf_op | source)
XLA Modules:
  0.0 76.8 jit_solution(12957721835793901310)
XLA Ops:
  1.9 21.1 %gather.1 = (bf16[16,272,128]{2,1,0:T(8,128)(2,1)S(1)}, bf16[3,272,128]{2,1,0:T(8,128)(2,1)S(1)}, s32[1,1,56]{2,1,0:T(1,128)S(1)}, s32[1,1,56]{2,1,0:T(1,128)S(1...) custom-call(s32[1,1]{1,0:T(1,128)S(6)} %copy.18.cnt_s, ...), custom_call_target="tpu_custom_call" | custom-call | tf_op jit(solution)/shard_map/gather/pallas_call | solution.py:332
  23.0 12.4 %pairs.1 = (bf16[16,272,128]{2,1,0:T(8,128)(2,1)S(1)}, f32[3,16,128]{2,1,0:T(8,128)S(1)}, f32[16,16,128]{2,1,0:T(8,128)S(1)}) custom-call(s32[1,1]{1,0:T(1,128)S(6)} %copy.19.refs_0_, bf16[3,272,128]{2,1,0:T(8,128)(2,1)S(1)} %get-tuple-element.26.refs_1_, bf16[16,272,128]{2,1,0:T(8,128)(2,1)S(1)} %get-tuple-element.27.refs_2_, ...), custom_call_target="tpu_custom_call" | custom-call | tf_op jit(solution)/shard_map/pairs/pallas_call | solution.py:230
  35.5 40.6 %reduce.1 = (f32[272,128]{1,0:T(8,128)S(1)}, f32[16,16,128]{2,1,0:T(8,128)S(1)}) custom-call(bf16[16,272,128]{2,1,0:T(8,128)(2,1)S(1)} %get-tuple-element.35.pack_ref, f32[3,16,128]{2,1,0:T(8,128)S(1)} %get-tuple-element.36.tg_ref, f32[16,16,128]{2,1,0:T(8,128)S(1)} %get-tuple-element.37.gw_ref), custom_call_target="tpu_custom_call" | custom-call | tf_op jit(solution)/shard_map/reduce/pallas_call | solution.py:398
  76.1 0.7 finish.1

commit v6 on v5

--- a/solution.py
+++ b/solution.py
@@ -60,8 +60,8 @@
     cnt_s,
     tower_ref, plate_ref, u_ref, v_ref, c_ref,
     wr_ref, br_ref, wf_ref, bf_ref,
-    pack_ref, tg_ref, gw_ref,
-    disp_ref, dist_ref, env_ref, tan_ref, dd_ref, rep_ref, gf_ref, list_ref, sum_ref, u_s, v_s, flag_ref, flag_s, order_s, list_sem,
+    gf_ref, sum_ref, disp_ref, dist_ref, dd_ref, list_ref,
+    env_ref, tan_ref, rep_ref, u_s, v_s, flag_ref, flag_s, order_s, list_sem,
     *, chunk, tiles,
 ):
     count = cnt_s[0, 0]
@@ -73,8 +73,6 @@
         list_ref[k:k + 1, 0:MAXT] = ref[0].astype(f32)
     lists = list_ref[...]
     columns = lists.T.astype(jnp.int32)
-    rrow = lists[0:1, 0:ROWS].astype(jnp.int32)
-    srow = lists[1:2, 0:ROWS].astype(jnp.int32)
     ucol = columns[0:ROWS, 0:1]
     vcol = columns[0:ROWS, 1:2]
     ccol = columns[0:ROWS, 2:3]
@@ -196,33 +194,6 @@
         order_s[kept + k] = ROWS - 1
     lax.fori_loop(0, (kept + tiles - 1) // tiles, body, 0)
 
-    radial = dd_ref[...] / dist_ref[...]
-    t_sum = jnp.zeros((48, F), f32)
-    p_sum = jnp.zeros((256, F), f32)
-    to_u = (rrow >> 3) * 16 + ((rrow >> 2) & 1) * 3
-    to_v = (srow >> 3) * 16 + ((srow >> 2) & 1) * 3
-    pulls = jnp.concatenate([part for d in range(3) for part in split(disp_ref[d] * radial)], axis=0)
-    recv_all = dot(pulls, rep4, NT)
-    send_all = dot(pulls, til4, NT)
-    for d in range(3):
-        at = 2 * ROWS * d
-        recv_hi, recv_lo = split(jnp.where(in_u, recv_all[at:at + ROWS] + recv_all[at + ROWS:at + 2 * ROWS], 0.0))
-        send_hi, send_lo = split(jnp.where(in_v, send_all[at:at + ROWS] + send_all[at + ROWS:at + 2 * ROWS], 0.0))
-        put_u = (to_u + d == iota((48, ROWS), 0)).astype(bf16)
-        put_v = (to_v + d == iota((256, ROWS), 0)).astype(bf16)
-        t_sum = t_sum + dot(put_u, recv_hi) + dot(put_u, recv_lo)
-        p_sum = p_sum - dot(put_v, send_hi) - dot(put_v, send_lo)
-    tg_ref[...] = t_sum.reshape(3, 16, F)
-    pack_ref[:, ATOMS:PACK, :] = p_sum.astype(bf16).reshape(BRICKS, 16, F)
-    pack_ref[:, 0:ATOMS, :] = gf_ref[...].reshape(BRICKS, ATOMS, F).astype(bf16)
-    gw_ref[0:8] = sum_ref[0:F, 0:F].T.reshape(8, WROWS, F)
-    gw_ref[8] = sum_ref[0:F, F:F + 2 * NRBF].T[0:WROWS]
-    rest = sum_ref[F:2 * F, F:F + 2 * NRBF].T
-    gw_ref[9] = rest[NRBF:2 * NRBF]
-    gw_ref[10] = rest[0:NRBF]
-    gw_ref[12:16] = jnp.zeros((4, WROWS, F), f32)
-    gw_ref[11] = jnp.full((WROWS, F), count, jnp.int32).astype(f32)
-
 
 def pairs(count, tower, plate, params, chunk=256, tiles=2):
     smem = pl.BlockSpec(memory_space=pltpu.SMEM)
@@ -230,22 +201,19 @@
     return pl.pallas_call(
         lambda *refs: pairs_kernel(*refs, chunk=chunk, tiles=tiles),
         out_shape=(
-            jax.ShapeDtypeStruct((BRICKS, PACK, F), bf16),
-            jax.ShapeDtypeStruct((3, 16, F), f32),
-            jax.ShapeDtypeStruct((16, WROWS, F), f32),
+            jax.ShapeDtypeStruct((PLATE, TILE, F), f32),
+            jax.ShapeDtypeStruct((2 * F, F + 2 * NRBF), f32),
+            jax.ShapeDtypeStruct((3, ROWS, PAIRS), f32),
+            jax.ShapeDtypeStruct((ROWS, PAIRS), f32),
+            jax.ShapeDtypeStruct((ROWS, PAIRS), f32),
+            jax.ShapeDtypeStruct((8, F), f32),
         ),
         in_specs=[smem] + [vmem] * 9,
-        out_specs=[vmem] * 3,
+        out_specs=[vmem] * 6,
         scratch_shapes=[
-            pltpu.VMEM((3, ROWS, PAIRS), f32),
-            pltpu.VMEM((ROWS, PAIRS), f32),
-            pltpu.VMEM((ROWS, PAIRS), f32),
             pltpu.VMEM((ROWS, PAIRS), f32),
             pltpu.VMEM((ROWS, PAIRS), f32),
             pltpu.VMEM((TILE, PAIRS), bf16),
-            pltpu.VMEM((PLATE, TILE, F), f32),
-            pltpu.VMEM((8, F), f32),
-            pltpu.VMEM((2 * F, F + 2 * NRBF), f32),
             pltpu.SMEM((1, 1, MAXT), jnp.int32),
             pltpu.SMEM((1, 1, MAXT), jnp.int32),
             pltpu.VMEM((8, ROWS), jnp.int32),
@@ -265,13 +233,6 @@
     )
     copy.start()
     return copy
-
-
-def greet(devices):
-    barrier = pltpu.get_barrier_semaphore()
-    for device in devices:
-        pl.semaphore_signal(barrier, inc=1, device_id=device, device_id_type=pl.DeviceIdType.MESH)
-    pl.semaphore_wait(barrier, len(devices))
 
 
 def gather_kernel(
@@ -343,9 +304,47 @@
     return out[0], out[1], out[2:]
 
 
+def prepare(count, gf_ref, sum_ref, disp_ref, dist_ref, dd_ref, list_ref, pack_ref, tg_ref, gw_ref):
+    gw_ref[0:8] = sum_ref[0:F, 0:F].T.reshape(8, WROWS, F)
+    gw_ref[8] = sum_ref[0:F, F:F + 2 * NRBF].T[0:WROWS]
+    rest = sum_ref[F:2 * F, F:F + 2 * NRBF].T
+    gw_ref[9] = rest[NRBF:2 * NRBF]
+    gw_ref[10] = rest[0:NRBF]
+    gw_ref[12:16] = jnp.zeros((4, WROWS, F), f32)
+    gw_ref[11] = jnp.full((WROWS, F), count, jnp.int32).astype(f32)
+    pack_ref[:, 0:ATOMS, :] = gf_ref[...].reshape(BRICKS, ATOMS, F).astype(bf16)
+    lists = list_ref[...]
+    columns = lists.T.astype(jnp.int32)
+    rows = lists[:, 0:ROWS].astype(jnp.int32)
+    group = iota((ROWS, F), 1) >> 5
+    in_u = group == (columns[0:ROWS, 0:1] & 3)
+    in_v = group == (columns[0:ROWS, 1:2] & 3)
+    rrow, srow = rows[0:1], rows[1:2]
+    rep4 = (iota((F, PAIRS), 1) >> 5 == (iota((F, PAIRS), 0) & 31)).astype(bf16)
+    til4 = ((iota((F, PAIRS), 1) & 31) == (iota((F, PAIRS), 0) & 31)).astype(bf16)
+    radial = dd_ref[...] / dist_ref[...]
+    t_sum = jnp.zeros((48, F), f32)
+    p_sum = jnp.zeros((256, F), f32)
+    to_u = (rrow >> 3) * 16 + ((rrow >> 2) & 1) * 3
+    to_v = (srow >> 3) * 16 + ((srow >> 2) & 1) * 3
+    pulls = jnp.concatenate([part for d in range(3) for part in split(disp_ref[d] * radial)], axis=0)
+    recv_all = dot(pulls, rep4, NT)
+    send_all = dot(pulls, til4, NT)
+    for d in range(3):
+        at = 2 * ROWS * d
+        recv_hi, recv_lo = split(jnp.where(in_u, recv_all[at:at + ROWS] + recv_all[at + ROWS:at + 2 * ROWS], 0.0))
+        send_hi, send_lo = split(jnp.where(in_v, send_all[at:at + ROWS] + send_all[at + ROWS:at + 2 * ROWS], 0.0))
+        put_u = (to_u + d == iota((48, ROWS), 0)).astype(bf16)
+        put_v = (to_v + d == iota((256, ROWS), 0)).astype(bf16)
+        t_sum = t_sum + dot(put_u, recv_hi) + dot(put_u, recv_lo)
+        p_sum = p_sum - dot(put_v, send_hi) - dot(put_v, send_lo)
+    tg_ref[...] = t_sum.reshape(3, 16, F)
+    pack_ref[:, ATOMS:PACK, :] = p_sum.astype(bf16).reshape(BRICKS, 16, F)
+
+
 def reduce_kernel(
-    pack_ref, tg_ref, gw_ref, acc_ref, w3_buf,
-    mate_buf, send_buf, chip_buf, tower_buf, w1_buf, w2_own, w2_buf,
+    cnt_s, gf_ref, sum_ref, disp_ref, dist_ref, dd_ref, list_ref, acc_ref, w3_buf,
+    pack_ref, tg_ref, gw_ref, mate_buf, send_buf, chip_buf, tower_buf, w1_buf, w2_own, w2_buf,
     mate_send, mate_recv, chip_send, chip_recv, tower_send, tower_recv, w_send, w_recv,
 ):
     t = lax.axis_index("tower")
@@ -355,7 +354,12 @@
     chips = [(q + d) % 8 for d in range(8)]
     plate = [(t, (p + d) % 16) for d in range(16)]
     tower = [((t + d) % 16, p) for d in range(16)]
-    greet(plate[1:] + tower[1:])
+    barrier = pltpu.get_barrier_semaphore()
+    peers = plate[1:] + tower[1:]
+    for device in peers:
+        pl.semaphore_signal(barrier, inc=1, device_id=device, device_id_type=pl.DeviceIdType.MESH)
+    prepare(cnt_s[0, 0], gf_ref, sum_ref, disp_ref, dist_ref, dd_ref, list_ref, pack_ref, tg_ref, gw_ref)
+    pl.semaphore_wait(barrier, len(peers))
     first = [send_to(gw_ref.at[(p + d) % 16], w1_buf.at[d], w_send.at[0], w_recv.at[0], d, plate[d]) for d in range(1, 16)]
     halves = [send_to(pack_ref.at[chips[d] * 2 + 1 - core], mate_buf.at[d], mate_send, mate_recv, d, mate) for d in (1, 2, 3, 4, 5, 6, 7, 0)]
     up = send_to(tg_ref.at[2], tower_buf.at[0], tower_send, tower_recv, 0, tower[1])
@@ -391,22 +395,23 @@
         copy.wait_send()
 
 
-def reduce(pack, tg, gw):
+def reduce(count, *partials):
+    smem = pl.BlockSpec(memory_space=pltpu.SMEM)
     vmem = pl.BlockSpec(memory_space=pltpu.VMEM)
     weights = pltpu.VMEM((16, WROWS, F), f32)
     dma = pltpu.SemaphoreType.DMA
     return pl.pallas_call(
         reduce_kernel,
         out_shape=(jax.ShapeDtypeStruct((PACK, F), f32), jax.ShapeDtypeStruct((16, WROWS, F), f32)),
-        in_specs=[vmem] * 3,
+        in_specs=[smem] + [vmem] * 6,
         out_specs=[vmem] * 2,
-        scratch_shapes=[pltpu.VMEM((8, PACK, F), bf16)] * 3 + [
+        scratch_shapes=[pltpu.VMEM((BRICKS, PACK, F), bf16), pltpu.VMEM((3, 16, F), f32), weights] + [pltpu.VMEM((8, PACK, F), bf16)] * 3 + [
             pltpu.VMEM((2, 16, F), f32), weights, pltpu.VMEM((WROWS, F), f32), weights,
             dma((8,)), dma((8,)), dma((8,)), dma((8,)), dma((2,)), dma((2,)), dma((3, 16)), dma((3, 16)),
         ],
         compiler_params=pltpu.CompilerParams(collective_id=1, has_side_effects=True, vmem_limit_bytes=24 << 20),
         name="reduce",
-    )(pack, tg, gw)
+    )(count, *partials)
 
 
 def finish_kernel(cnt_s, acc_ref, w_ref, gf_out, gp_out, wr_out, br_out, wf_out, bf_out):
@@ -440,8 +445,8 @@
 def local(features, adjoint, positions, w_rbf, b_rbf, w_filter, b_filter, atom_counts, tile_counts, tower_tiles, plate_tiles, image_shifts):
     params = [pltpu.with_memory_space_constraint(x, pltpu.HBM) for x in (tower_tiles, plate_tiles, image_shifts, w_rbf, b_rbf.reshape(1, F), w_filter, b_filter.reshape(1, F))]
     plate, tower, params = gather(atom_counts, *[pltpu.with_memory_space_constraint(x, pltpu.HBM) for x in (features[0], adjoint[0], positions[:, 0, :])], params)
-    pack, tg, gw = pairs(tile_counts, tower, plate, params)
-    gf, gp, wr, br, wf, bf = finish(atom_counts, *reduce(pack, tg, gw))
+    partials = pairs(tile_counts, tower, plate, params)
+    gf, gp, wr, br, wf, bf = finish(atom_counts, *reduce(tile_counts, *partials))
     return gf, gp, wr, br[0], wf, bf[0]
 
 

time: 76.9 us -> 73.2 us (0.952)
  Pallas kernels: 74.8 us -> 71.1 us
    pallas_call x1, Pallas kernels: 12.4 us -> 9.3 us  [pairs(): pl.pallas_call(lambda *refs: pairs_kernel(*refs, chunk=chunk, tiles=tiles...]
where the time goes in v6:
time: 73.2 us; the launch traced here: 73 us
  Pallas kernels  71.1 us (97%)
  between operations  1.95 us (3%)
    pallas_call x1, Pallas kernels, reduce(): pl.pallas_call(reduce_kernel, out_shape=(jax.ShapeDtypeStruct((PACK, F),...  40 us
    pallas_call x1, Pallas kernels, gather(): pl.pallas_call(gather_kernel, out_shape=[jax.ShapeDtypeStruct((BRICKS, PA...  21.1 us
    pallas_call x1, Pallas kernels, pairs(): pl.pallas_call(lambda *refs: pairs_kernel(*refs, chunk=chunk, tiles=tiles...  9.3 us

profile of v6, /device:TPU:1, one launch (start us, length us, event | category | flops | bytes accessed | tf_op | source)
XLA Modules:
  0.0 73.0 jit_solution(2400841024211347888)
XLA Ops:
  1.9 21.1 %gather.1 = (bf16[16,272,128]{2,1,0:T(8,128)(2,1)S(1)}, bf16[3,272,128]{2,1,0:T(8,128)(2,1)S(1)}, s32[1,1,56]{2,1,0:T(1,128)S(1)}, s32[1,1,56]{2,1,0:T(1,128)S(1...) custom-call(s32[1,1]{1,0:T(1,128)S(6)} %copy.18.cnt_s, ...), custom_call_target="tpu_custom_call" | custom-call | tf_op jit(solution)/shard_map/gather/pallas_call | solution.py:293
  23.0 9.3 %pairs.1 = (f32[128,32,128]{2,1,0:T(8,128)S(1)}, f32[256,160]{1,0:T(8,128)S(1)}, f32[3,64,1024]{2,1,0:T(8,128)S(1)}, f32[64,1024]{1,0:T(8,128)S(1)}, f32[64,1024]{1,0:T(8,128)S(1)}, /*index=5*/f32[8,128]{1,0:T(8,128)S(1)}) custom-call(s32[1,1]{1,0:T(1,128)S(6)} %copy.19.refs_0_.cnt_s, bf16[3,272,128]{2,1,0:T(8,128)(2,1)S(1)} %get-tuple-element.29.refs_1_, ...), custom_call_target="tpu_custom_call" | custom-call | tf_op jit(solution)/shard_map/pairs/pallas_call | solution.py:201
  32.4 40.0 %reduce.1 = (f32[272,128]{1,0:T(8,128)S(1)}, f32[16,16,128]{2,1,0:T(8,128)S(1)}) custom-call(s32[1,1]{1,0:T(1,128)S(6)} %copy.19.refs_0_.cnt_s, f32[128,32,128]{2,1,0:T(8,128)S(1)} %get-tuple-element.38.gf_ref, f32[256,160]{1,0:T(8,128)S(1)} %get-tuple-element.39.sum_ref, f32[3,64,1024]{2,1,0:T(8,128)S(1)} %get-tuple-element.40.disp_ref, ...), custom_call_target="tpu_custom_call" | custom-call | tf_op jit(solution)/shard_map/reduce/pallas_call | solution.py:403
  72.3 0.7 finish.1

commit v7 on v6

--- a/solution.py
+++ b/solution.py
@@ -127,8 +127,7 @@
     hwf = (wf * 0.5).astype(bf16)
     fold = ((iota((TILE, 2 * F), 1) & 31) == iota((TILE, 2 * F), 0)).astype(bf16)
 
-    def body(step, carry):
-        entries = [order_s[step * tiles + k] for k in range(tiles)]
+    def visit(entries, group):
         streams = []
         for e in entries:
             listed = jnp.minimum(e, MAXT - 1)
@@ -141,7 +140,8 @@
             wide = jnp.concatenate([feat4] * (chunk // F), axis=1)
             for s in range(0, PAIRS, chunk):
                 streams.append(dict(e=e, v=v, adj=adj, wide=wide, lanes=pl.ds(s, chunk)))
-        for x in streams:
+
+        def opening(x):
             x['off'] = dist_ref[pl.ds(x['e'], 1), x['lanes']] - centres
             x['basis'] = jnp.exp(-sharp * x['off'] * x['off'])
             x['inputs'] = jnp.concatenate([x['basis'].astype(bf16), ones], axis=0)
@@ -150,25 +150,35 @@
             member = rep_ref[:, x['lanes']]
             spread = jnp.concatenate([member * hi, member * lo], axis=0)
             x['adj_env'] = dot(x['adj'], spread, TN)
-        for x in streams:
+
+        def middle(x):
             x['t'] = jnp.tanh(x['half'])
             x['soft_b'] = jnp.concatenate([jnp.log(1.0 - x['t']).astype(bf16), ones], axis=0)
             x['d_raw_b'] = (x['adj_env'] * x['wide']).astype(bf16)
-        for x in streams:
             x['filt'] = dot(nwft, x['soft_b'])
             x['d_soft'] = dot(hwf, x['d_raw_b'])
-        for x in streams:
+
+        def closing(x):
             x['d_pre_b'] = (x['d_soft'] * (1.0 + x['t'])).astype(bf16)
             x['y'] = x['adj_env'] * x['filt']
-            x['zsum'] = jnp.sum(x['y'] * x['wide'], axis=0, keepdims=True)
-        gw = jnp.zeros((2 * F, F + 2 * NRBF), f32)
-        for x in streams:
+            zsum = jnp.sum(x['y'] * x['wide'], axis=0, keepdims=True)
             d_basis = dot(wr, x['d_pre_b'])
-            d_dist = jnp.sum(d_basis * x['basis'] * x['off'], axis=0, keepdims=True) * (-2.0 * sharp)
-            x['dd'] = d_dist + tan_ref[pl.ds(x['e'], 1), x['lanes']] * x['zsum']
             grads = jnp.concatenate([x['d_raw_b'], x['d_pre_b']], axis=0)
             values = jnp.concatenate([x['soft_b'], x['inputs'][0:NRBF]], axis=0)
-            gw = gw + dot(grads, values, NT)
+            x['gw'] = dot(grads, values, NT)
+            d_dist = jnp.sum(d_basis * x['basis'] * x['off'], axis=0, keepdims=True) * (-2.0 * sharp)
+            x['dd'] = d_dist + tan_ref[pl.ds(x['e'], 1), x['lanes']] * zsum
+
+        stages = (opening, middle, closing)
+        groups = [streams[i:i + group] for i in range(0, len(streams), group)]
+        for tick in range(len(groups) + len(stages) - 1):
+            for lag, stage in enumerate(stages):
+                if 0 <= tick - lag < len(groups):
+                    for x in groups[tick - lag]:
+                        stage(x)
+        gw = streams[0]['gw']
+        for x in streams[1:]:
+            gw = gw + x['gw']
         for e in entries:
             acc = jnp.zeros((F, F), f32)
             for x in streams:
@@ -179,7 +189,6 @@
                         acc = acc + x['y'][:, q:q + F]
             gf_ref[v] += dot(fold, jnp.concatenate(split(acc), axis=1), NT)
         sum_ref[...] += gw
-        return carry
 
     for copy in lists_in:
         copy.wait()
@@ -190,12 +199,22 @@
         return n + flag_s[0, e]
 
     kept = lax.fori_loop(0, MAXT, keep, 0)
-    for k in range(tiles - 1):
-        order_s[kept + k] = ROWS - 1
-    lax.fori_loop(0, (kept + tiles - 1) // tiles, body, 0)
-
-
-def pairs(count, tower, plate, params, chunk=256, tiles=2):
+    order_s[kept] = ROWS - 1
+    whole = kept // tiles
+
+    def many(step, carry):
+        visit([order_s[step * tiles + k] for k in range(tiles)], 1024 // chunk)
+        return carry
+
+    def two(step, carry):
+        visit([order_s[whole * tiles + 2 * step + k] for k in range(2)], 2 * PAIRS // chunk)
+        return carry
+
+    lax.fori_loop(0, whole, many, 0)
+    lax.fori_loop(0, (kept - whole * tiles + 1) // 2, two, 0)
+
+
+def pairs(count, tower, plate, params, chunk=256, tiles=7):
     smem = pl.BlockSpec(memory_space=pltpu.SMEM)
     vmem = pl.BlockSpec(memory_space=pltpu.VMEM)
     return pl.pallas_call(

time: 73.2 us -> 73 us (level)
    pallas_call x1, Pallas kernels: 40 us -> 39.2 us  [reduce(): pl.pallas_call(reduce_kernel, out_shape=(jax.ShapeDtypeStruct((PACK, F),...]
where the time goes in v7:
time: 73 us; the launch traced here: 72.5 us
  Pallas kernels  70.6 us (97%)
  between operations  1.95 us (3%)
    pallas_call x1, Pallas kernels, reduce(): pl.pallas_call(reduce_kernel, out_shape=(jax.ShapeDtypeStruct((PACK, F),...  39.2 us
    pallas_call x1, Pallas kernels, gather(): pl.pallas_call(gather_kernel, out_shape=[jax.ShapeDtypeStruct((BRICKS, PA...  21.1 us
    pallas_call x1, Pallas kernels, pairs(): pl.pallas_call(lambda *refs: pairs_kernel(*refs, chunk=chunk, tiles=tiles...  9.61 us

profile of v7, /device:TPU:1, one launch (start us, length us, event | category | flops | bytes accessed | tf_op | source)
XLA Modules:
  0.0 72.5 jit_solution(9309360273232870157)
XLA Ops:
  1.9 21.1 %gather.1 = (bf16[16,272,128]{2,1,0:T(8,128)(2,1)S(1)}, bf16[3,272,128]{2,1,0:T(8,128)(2,1)S(1)}, s32[1,1,56]{2,1,0:T(1,128)S(1)}, s32[1,1,56]{2,1,0:T(1,128)S(1...) custom-call(s32[1,1]{1,0:T(1,128)S(6)} %copy.18.cnt_s, ...), custom_call_target="tpu_custom_call" | custom-call | tf_op jit(solution)/shard_map/gather/pallas_call | solution.py:312
  23.0 9.6 %pairs.1 = (f32[128,32,128]{2,1,0:T(8,128)S(1)}, f32[256,160]{1,0:T(8,128)S(1)}, f32[3,64,1024]{2,1,0:T(8,128)S(1)}, f32[64,1024]{1,0:T(8,128)S(1)}, f32[64,1024]{1,0:T(8,128)S(1)}, /*index=5*/f32[8,128]{1,0:T(8,128)S(1)}) custom-call(s32[1,1]{1,0:T(1,128)S(6)} %copy.19.refs_0_.cnt_s, bf16[3,272,128]{2,1,0:T(8,128)(2,1)S(1)} %get-tuple-element.29.refs_1_, ...), custom_call_target="tpu_custom_call" | custom-call | tf_op jit(solution)/shard_map/pairs/pallas_call | solution.py:220
  32.7 39.2 %reduce.1 = (f32[272,128]{1,0:T(8,128)S(1)}, f32[16,16,128]{2,1,0:T(8,128)S(1)}) custom-call(s32[1,1]{1,0:T(1,128)S(6)} %copy.19.refs_0_.cnt_s, f32[128,32,128]{2,1,0:T(8,128)S(1)} %get-tuple-element.38.gf_ref, f32[256,160]{1,0:T(8,128)S(1)} %get-tuple-element.39.sum_ref, f32[3,64,1024]{2,1,0:T(8,128)S(1)} %get-tuple-element.40.disp_ref, ...), custom_call_target="tpu_custom_call" | custom-call | tf_op jit(solution)/shard_map/reduce/pallas_call | solution.py:422
  71.8 0.7 finish.1
